TPU v7x, 128 devices: a whole 4x4x4 slice. The times are simulated.
128 devices in a mesh: dom: 16 (over x, y_hi, core), phase: 2 (over y_lo), feat: 4 (over z).
Axes of the slice: x: 4, y: 4 (y_hi: 2, y_lo: 2; y = y_hi * 2 + y_lo), z: 4, core: 2. Of those that a mesh axis runs over, the one named last changes fastest.
Arguments:
- node_in: bfloat16 [524288, 256], P(('dom', 'phase', 'feat')), may hold values from -6 to 6
- out_cot: bfloat16 [524288, 256], P(('dom', 'phase', 'feat')), may hold values from -6 to 6
- adjacency: bfloat16 [4096, 4, 128, 128], P(('dom', 'phase', 'feat')), may hold values from -0.25 to 0.25
- tile_nbrs: int32 [4096, 4], P(('dom', 'phase', 'feat')), may hold values from 0 to 47, as said below
- bound_tiles: int32 [128, 2, 8], P(('dom', 'phase', 'feat')), may hold values from 0 to 15, as said below
- live_tiles: int32 [128], P(('dom', 'phase', 'feat')), may hold values from 16 to 32, as said below
- w_self: bfloat16 [2, 256, 256], replicated, may hold values from -0.25 to 0.25
- w_nbr: bfloat16 [2, 256, 256], replicated, may hold values from -0.25 to 0.25
- pre_bias: float32 [2, 256], replicated, may hold values from -3 to 3
- w_out: bfloat16 [2, 256, 256], replicated, may hold values from -0.375 to 0.375
Outputs:
- section_out: bfloat16 [2, 524288, 256], P(None, ('dom', 'phase', 'feat'))
- section_in_grad: bfloat16 [2, 524288, 256], P(None, ('dom', 'phase', 'feat'))
- grad_self: float32 [2, 256, 256], replicated
- grad_nbr: float32 [2, 256, 256], replicated
- grad_bias: float32 [2, 256], replicated
- grad_out: float32 [2, 256, 256], replicated
Inputs may be any that keep to these rules, and one draw needn't show every extreme that they name: `live_tiles`: some partition has all 32 tiles live. `bound_tiles`: for each partition the 16 entries are the tiles 0 to 15, each once. `tile_nbrs`: slot 0 of local tile i is i; every entry of a live tile names a live own tile (below 32) or an extended tile (from 32 on); each extended tile is named by some live tile; all entries of a tile that is not live are i.
All inputs are finite; a program needn't handle non-finite values.
Results may differ from a plain program's by a relative error of at most 0.008.
Values may be sent and summed in bfloat16 or wider, within the bound.
A program may use at most 192 MiB of HBM per device.

v0:
```python
import jax
import jax.numpy as jnp
from jax import lax
from jax.sharding import PartitionSpec as P


def passed_along(value, axis, steps):
    count = lax.axis_size(axis)
    pairs = [(source, (source + steps) % count) for source in range(count)]
    return lax.ppermute(value, axis, pairs)


def silu_slope(pre_act):
    sigma = jax.nn.sigmoid(pre_act)
    return sigma * (1.0 + pre_act * (1.0 - sigma))


def extend_tiles(node_tiles, bound_idx):
    west_send = node_tiles[bound_idx[0]]
    east_send = node_tiles[bound_idx[1]]
    from_west = passed_along(east_send, ("dom", "phase", "feat"), 1)
    from_east = passed_along(west_send, ("dom", "phase", "feat"), -1)
    return jnp.concatenate([node_tiles, from_west, from_east], axis=0)


def return_back(collected, bound_idx):
    edge_count = bound_idx.shape[1]
    tile_count = collected.shape[0] - 2 * edge_count
    west_part = collected[tile_count : tile_count + edge_count]
    east_part = collected[tile_count + edge_count :]
    from_east = passed_along(west_part.astype(jnp.bfloat16), ("dom", "phase", "feat"), -1).astype(
        west_part.dtype
    )
    from_west = passed_along(east_part.astype(jnp.bfloat16), ("dom", "phase", "feat"), 1).astype(
        east_part.dtype
    )
    local_part = collected[:tile_count].at[bound_idx[1]].add(from_east)
    return local_part.at[bound_idx[0]].add(from_west)


def forward(features, weights, graph_data):
    w_self, w_nbr, pre_bias, w_out = weights
    adjacency, neighbours, bound_idx, mask_rows = graph_data
    tile_count, tile_rows = (adjacency.shape[0], adjacency.shape[2])
    node_tiles = features.reshape(tile_count, tile_rows, -1)
    extended = extend_tiles(node_tiles, bound_idx)
    picked = extended[neighbours]
    summed = jnp.einsum("tkij,tkjc->tic", adjacency, picked, preferred_element_type=jnp.float32)
    gathered = summed.reshape(features.shape).astype(jnp.bfloat16)
    pre_act = (
        jnp.dot(features, w_self, preferred_element_type=jnp.float32)
        + jnp.dot(gathered, w_nbr, preferred_element_type=jnp.float32)
        + pre_bias
    )
    hidden = jax.nn.silu(pre_act).astype(jnp.bfloat16)
    result = (
        mask_rows
        * (
            features.astype(jnp.float32)
            + jnp.dot(hidden, w_out, preferred_element_type=jnp.float32)
        )
    ).astype(jnp.bfloat16)
    return (result, (features, gathered, pre_act, hidden))


def backward(upstream, saved_state, weights, graph_data):
    w_self, w_nbr, pre_bias, w_out = weights
    adjacency, neighbours, bound_idx, mask_rows = graph_data
    features, gathered, pre_act, hidden = saved_state
    tile_count, slot_count, tile_rows = (adjacency.shape[0], adjacency.shape[1], adjacency.shape[2])
    edge_count = bound_idx.shape[1]
    masked = upstream * mask_rows.astype(jnp.bfloat16)
    grad_out = jnp.dot(hidden.T, masked, preferred_element_type=jnp.float32)
    grad_hidden = jnp.dot(masked, w_out.T, preferred_element_type=jnp.float32)
    grad_pre = (grad_hidden * silu_slope(pre_act)).astype(jnp.bfloat16)
    grad_self = jnp.dot(features.T, grad_pre, preferred_element_type=jnp.float32)
    grad_nbr = jnp.dot(gathered.T, grad_pre, preferred_element_type=jnp.float32)
    grad_bias = jnp.sum(grad_pre, axis=0, dtype=jnp.float32)
    direct = masked.astype(jnp.float32) + jnp.dot(
        grad_pre, w_self.T, preferred_element_type=jnp.float32
    )
    grad_gathered = jnp.dot(grad_pre, w_nbr.T, preferred_element_type=jnp.float32).astype(
        jnp.bfloat16
    )
    contrib = jnp.einsum(
        "tkij,tic->tkjc",
        adjacency,
        grad_gathered.reshape(tile_count, tile_rows, -1),
        preferred_element_type=jnp.float32,
    )
    collected = jax.ops.segment_sum(
        contrib.reshape(tile_count * slot_count, tile_rows, -1),
        neighbours.reshape(-1),
        num_segments=tile_count + 2 * edge_count,
    )
    returned = return_back(collected, bound_idx)
    grad_in = (direct + returned.reshape(direct.shape)).astype(jnp.bfloat16)
    return (grad_in, (grad_self, grad_nbr, grad_bias, grad_out))


def per_device(
    node_in, out_cot, adjacency, tile_nbrs, bound_tiles, live_tiles, w_self, w_nbr, pre_bias, w_out
):
    tile_count, tile_rows = (adjacency.shape[0], adjacency.shape[2])
    alive_tiles = (jnp.arange(tile_count) < live_tiles[0]).astype(jnp.float32)
    mask_rows = jnp.repeat(alive_tiles, tile_rows)[:, None]
    graph_data = (adjacency, tile_nbrs, bound_tiles[0], mask_rows)
    first_weights = (w_self[0], w_nbr[0], pre_bias[0], w_out[0])
    second_weights = (w_self[1], w_nbr[1], pre_bias[1], w_out[1])
    first_out, first_saved = forward(node_in, first_weights, graph_data)
    second_out, second_saved = forward(first_out, second_weights, graph_data)
    grad_mid, later = backward(out_cot, second_saved, second_weights, graph_data)
    grad_first, early = backward(grad_mid, first_saved, first_weights, graph_data)
    summed_all = lax.psum(
        (early[0], early[1], early[2], early[3], later[0], later[1], later[2], later[3]),
        ("dom", "phase", "feat"),
    )
    early_sum = summed_all[:4]
    later_sum = summed_all[4:]
    section_out = jnp.stack([first_out, second_out])
    section_in_grad = jnp.stack([grad_first, grad_mid])
    grad_self = jnp.stack([early_sum[0], later_sum[0]])
    grad_nbr = jnp.stack([early_sum[1], later_sum[1]])
    grad_bias = jnp.stack([early_sum[2], later_sum[2]])
    grad_out = jnp.stack([early_sum[3], later_sum[3]])
    return (section_out, section_in_grad, grad_self, grad_nbr, grad_bias, grad_out)


def solution(mesh):
    in_specs = (
        P(("dom", "phase", "feat"), None),
        P(("dom", "phase", "feat"), None),
        P(("dom", "phase", "feat"), None, None, None),
        P(("dom", "phase", "feat"), None),
        P(("dom", "phase", "feat"), None, None),
        P(("dom", "phase", "feat")),
        P(),
        P(),
        P(),
        P(),
    )
    out_specs = (
        P(None, ("dom", "phase", "feat"), None),
        P(None, ("dom", "phase", "feat"), None),
        P(),
        P(),
        P(),
        P(),
    )
    return jax.shard_map(
        per_device, mesh=mesh, in_specs=in_specs, out_specs=out_specs, check_vma=False
    )
```

profile of v0, /device:TPU:1, one launch (start us, length us, event | category | flops | bytes accessed | tf_op | source)
XLA Modules:
  0.0 452.4 jit_solution(10428271576731698897)
XLA Ops:
  8.1 3.0 gather_fusion
  11.0 2.5 collective-permute-start
  13.5 3.0 gather_fusion.1
  16.5 3.7 collective-permute-start.1
  23.4 3.6 fusion.40
  27.1 1.7 collective-permute-done
  28.8 1.9 collective-permute-done.1
  30.7 1.8 pad_maximum_fusion.2
  32.6 8.5 %gather_fusion.2 = bf16[128,128,256]{2,1,0:T(8,128)(2,1)} fusion(bf16[48,128,256]{2,1,0:T(8,128)(2,1)} %pad_maximum_fusion.2, s32[1024]{0:T(1024)S(1)} %pad_clamp_fusion), kind=kCustom, calls=%fused_computation.2 | custom fusion | bytes 16777728 | tf_op jit(solution)/shard_map/gather | solution.py:47
  41.1 6.4 %bitcast_convert_fusion.1 = bf16[32,256,128]{1,2,0:T(8,128)(2,1)S(1)} fusion(bf16[32,4,128,128]{3,2,1,0:T(8,128)(2,1)} %param.12, bf16[32,4,128,256]{3,2,1,0:T(8,128)(2,1)} %bitcast.154), kind=kOutput, calls=%fused_computation.38 | convolution fusion | flops 1074790400 | bytes 14680064 | tf_op jit(solution)/shard_map/tkij,tkjc->tic/dot_general | solution.py:48
  47.5 3.3 multiply_convert_fusion.1
  53.5 5.5 %collective-permute-start.3 = (bf16[8,128,256]{2,1,0:T(8,128)(2,1)S(1)}, bf16[8,128,256]{2,1,0:T(8,128)(2,1)S(1)}, u32[]{:S(2)}, u32[]{:S(2)}) collective-permute-start(bf16[8,128,256]{2,1,0:T(8,128)(2,1)S(1)} %gather_fusion.4), channel_id=1, source_target_pairs={{0,127},{1,0},{2,1},{3,2},{4,3},{5,4},{6,5},{7,6},{8,7},{9,8},{10,... | collective-permute-start | bytes 1572872 | tf_op jit(solution)/shard_map/ppermute | solution.py:10
  59.0 2.7 fusion.33
  61.7 7.5 %collective-permute-done.2 = bf16[8,128,256]{2,1,0:T(8,128)(2,1)S(1)} collective-permute-done((bf16[8,128,256]{2,1,0:T(8,128)(2,1)S(1)}, bf16[8,128,256]{2,1,0:T(8,128)(2,1)S(1)}, u32[]{:S(2)}, u32[]{:S(2)}) %collective-permute-start.2) | collective-permute-done | bytes 524320 | tf_op jit(solution)/shard_map/ppermute | solution.py:10
  69.2 2.3 pad_maximum_fusion.3
  71.6 8.5 %gather_fusion.5 = bf16[128,128,256]{2,1,0:T(8,128)(2,1)} fusion(bf16[48,128,256]{2,1,0:T(8,128)(2,1)} %pad_maximum_fusion.3, s32[1024]{0:T(1024)S(1)} %pad_clamp_fusion), kind=kCustom, calls=%fused_computation.5 | custom fusion | bytes 16777728 | tf_op jit(solution)/shard_map/gather | solution.py:47
  80.1 6.4 %bitcast_convert_fusion = bf16[32,256,128]{1,2,0:T(8,128)(2,1)S(1)} fusion(bf16[32,4,128,128]{3,2,1,0:T(8,128)(2,1)} %param.12, bf16[32,4,128,256]{3,2,1,0:T(8,128)(2,1)} %bitcast.153), kind=kOutput, calls=%fused_computation.37 | convolution fusion | flops 1074790400 | bytes 14680064 | tf_op jit(solution)/shard_map/tkij,tkjc->tic/dot_general | solution.py:48
  86.5 2.7 multiply_convert_fusion
  89.2 3.4 convert_reduce_fusion
  96.1 8.1 %fusion.59 = f32[32,256,4,128]{3,1,2,0:T(8,128)} fusion(bf16[32,128,256,1]{2,1,3,0:T(8,128)(2,1)S(1)} %bitcast.159, bf16[32,4,128,128]{3,2,1,0:T(8,128)(2,1)S(1)} %copy-done.1), kind=kOutput, calls=%fused_computation.108 | convolution fusion | flops 1073741824 | bytes 23068672 | tf_op jit(solution)/shard_map/tkij,tic->tkjc/dot_general | solution.py:85
  104.2 17.4 %copy.27 = f32[128,128,256]{2,1,0:T(8,128)} copy(f32[128,128,256]{1,2,0:T(8,128)} %bitcast.151) | data formatting | bytes 33554432 | tf_op jit(solution)/shard_map/reshape | solution.py:92
  121.7 3.4 broadcast.51.clone
  125.1 36.7 %scatter_fusion = f32[48,128,256]{2,1,0:T(8,128)} fusion(f32[48,128,256]{2,1,0:T(8,128)} %broadcast.51.clone, s32[128]{0:T(128)S(1)} %reshape.168, f32[128,128,256]{2,1,0:T(8,128)} %copy.27), kind=kCustom, calls=%fused_computation.6 | custom fusion | flops 4194304 | bytes 50332160 | tf_op jit(solution)/shard_map/scatter-add | solution.py:91
  161.7 3.4 convert.8
  166.0 5.7 %collective-permute-start.4 = (bf16[8,128,256]{2,1,0:T(8,128)(2,1)S(1)}, bf16[8,128,256]{2,1,0:T(8,128)(2,1)S(1)}, u32[]{:S(2)}, u32[]{:S(2)}) collective-permute-start(bf16[8,128,256]{2,1,0:T(8,128)(2,1)S(1)} %get-tuple-element.29), channel_id=1, source_target_pairs={{0,127},{1,0},{2,1},{3,2},{4,3},{5,4},{6,5},{7,6},{8,7},{9,8},{10,... | collective-permute-start | bytes 1572872 | tf_op jit(solution)/shard_map/ppermute | solution.py:10
  171.9 2.0 fusion.8
  173.9 1.7 convolution_bitcast_fusion.2
  175.6 2.4 slice.88
  178.0 2.1 fusion.18
  181.6 3.3 scatter_fusion.1
  186.1 3.3 scatter_fusion.2
  189.4 4.6 %fusion.10 = bf16[4096,256]{1,0:T(8,128)(2,1)S(1)} fusion(f32[32,128,256]{2,1,0:T(8,128)} %scatter_fusion.2, bf16[4096,256]{1,0:T(8,128)(2,1)} %copy-done.11, bf16[4096,256]{1,0:T(8,128)(2,1)} %param.11, bf16[4096]{0:T(1024)(128)(2,1)S(1)} %bitcast_convert_fusion.2, bf16[2,256,256]{2,1,0:T(8,128)(2,1)S(1)} %copy-done.23), kind=kOutput, calls=%fused_computation.36 | convolution fusion | flops 542113792 | bytes 10625024 | tf_op jit(solution)/shard_map/dot_general | solution.py:79
  194.2 3.3 convert_reduce_fusion.1
  201.2 8.1 %fusion.60 = f32[32,256,4,128]{3,1,2,0:T(8,128)} fusion(bf16[32,128,256,1]{2,1,3,0:T(8,128)(2,1)S(1)} %bitcast.160, bf16[32,4,128,128]{3,2,1,0:T(8,128)(2,1)S(1)} %copy-done.2), kind=kOutput, calls=%fused_computation.109 | convolution fusion | flops 1073741824 | bytes 23068672 | tf_op jit(solution)/shard_map/tkij,tic->tkjc/dot_general | solution.py:85
  209.3 17.4 %copy.29 = f32[128,128,256]{2,1,0:T(8,128)} copy(f32[128,128,256]{1,2,0:T(8,128)} %bitcast.152) | data formatting | bytes 33554432 | tf_op jit(solution)/shard_map/reshape | solution.py:92
  226.7 3.4 broadcast.51
  230.1 36.8 %scatter_fusion.3 = f32[48,128,256]{2,1,0:T(8,128)} fusion(f32[48,128,256]{2,1,0:T(8,128)} %broadcast.51, s32[128]{0:T(128)S(1)} %reshape.168, f32[128,128,256]{2,1,0:T(8,128)} %copy.29), kind=kCustom, calls=%fused_computation.9 | custom fusion | flops 4194304 | bytes 50332160 | tf_op jit(solution)/shard_map/scatter-add | solution.py:91
  267.0 3.4 convert.9
  271.3 5.8 %collective-permute-start.6 = (bf16[8,128,256]{2,1,0:T(8,128)(2,1)S(1)}, bf16[8,128,256]{2,1,0:T(8,128)(2,1)}, u32[]{:S(2)}, u32[]{:S(2)}) collective-permute-start(bf16[8,128,256]{2,1,0:T(8,128)(2,1)S(1)} %get-tuple-element.27), channel_id=1, source_target_pairs={{0,127},{1,0},{2,1},{3,2},{4,3},{5,4},{6,5},{7,6},{8,7},{9,8},{10,... | collective-permute-start | bytes 1572872 | tf_op jit(solution)/shard_map/ppermute | solution.py:10
  278.6 2.5 slice.91
  282.3 2.1 fusion.21
  284.4 69.5 %all-reduce = (f32[1,256]{1,0:T(1,128)S(1)}, f32[1,256]{1,0:T(1,128)S(1)}) all-reduce(f32[1,256]{1,0:T(1,128)S(1)} %bitcast.165, f32[1,256]{1,0:T(1,128)S(1)} %bitcast.166), channel_id=1, replica_groups=mesh['dom'=16,'phase'=2,'feat'=4] {'dom','phase','feat'}, use_global_device_ids=true, to_apply=%region_13.14 | all-reduce | flops 512 | bytes 4096 | tf_op jit(solution)/shard_map/psum | solution.py:114
  355.6 3.3 scatter_fusion.4
  360.1 3.3 scatter_fusion.5
  363.4 4.6 %fusion.11 = bf16[1,4096,256]{2,1,0:T(8,128)(2,1)S(1)} fusion(f32[32,128,256]{2,1,0:T(8,128)} %scatter_fusion.5, bf16[4096,256]{1,0:T(8,128)(2,1)} %copy-done.9, bf16[4096,256]{1,0:T(8,128)(2,1)} %copy-done.6, bf16[4096]{0:T(1024)(128)(2,1)S(1)} %bitcast_convert_fusion.2, bf16[2,256,256]{2,1,0:T(8,128)(2,1)S(1)} %copy-done.23), kind=kOutput, calls=%fused_computation.41 | convolution fusion | flops 542113792 | bytes 10625024 | tf_op jit(solution)/shard_map/dot_general | solution.py:79
  368.1 3.7 pad_maximum_fusion
  371.8 69.3 %all-reduce.4.cloned.1.call-done = (f32[1,256,256]{1,2,0:T(8,128)}, f32[1,256,256]{1,2,0:T(8,128)}, f32[1,256,256]{2,1,0:T(8,128)}, f32[1,256,256]{2,1,0:T(8,128...) async-done(((f32[1,256,256]{1,2,0:T(8,128)}, f32[1,256,256]{1,2,0:T(8,128)}, f32[1,256,256]{2,1,0:T(8,128)}, f32[1,256,256]{2,1,0:T(8,128)}, f32[1,256,256]{2,1,0:T(8,128)}, ...) | async-done | bytes 1572880 | tf_op jit(solution)/shard_map/psum | solution.py:114
  443.1 2.2 pad_maximum_fusion.5
  (107 shorter events, 25.9 us)
Async XLA Ops:
  7.2 16.3 %copy-start.3 = (bf16[4096,256]{1,0:T(8,128)(2,1)S(1)}, bf16[4096,256]{1,0:T(8,128)(2,1)}, u32[]{:S(2)}) copy-start(bf16[4096,256]{1,0:T(8,128)(2,1)} %param.10) | copy-start | bytes 6291460
  7.2 433.8 %all-reduce.4.cloned.1.call-start = ((), (), s32[]{:S(2)}) async-start(), calls=%async_computation | async-start | bytes 3145728 | tf_op jit(solution)/shard_map/psum | solution.py:114
  11.0 17.7 %collective-permute-start = (bf16[8,128,256]{2,1,0:T(8,128)(2,1)}, bf16[8,128,256]{2,1,0:T(8,128)(2,1)S(1)}, u32[]{:S(2)}, u32[]{:S(2)}) collective-permute-start(bf16[8,128,256]{2,1,0:T(8,128)(2,1)} %gather_fusion), channel_id=1, source_target_pairs={{0,1},{1,2},{2,3},{3,4},{4,5},{5,6},{6,7},{7,8},{8,9},{9,10},{10,1... | collective-permute-start | bytes 1572872 | tf_op jit(solution)/shard_map/ppermute | solution.py:10
  16.5 14.3 %collective-permute-start.1 = (bf16[8,128,256]{2,1,0:T(8,128)(2,1)}, bf16[8,128,256]{2,1,0:T(8,128)(2,1)S(1)}, u32[]{:S(2)}, u32[]{:S(2)}) collective-permute-start(bf16[8,128,256]{2,1,0:T(8,128)(2,1)} %gather_fusion.1), channel_id=1, source_target_pairs={{0,127},{1,0},{2,1},{3,2},{4,3},{5,4},{6,5},{7,6},{8,7},{9,8},{10,... | collective-permute-start | bytes 1572872 | tf_op jit(solution)/shard_map/ppermute | solution.py:10
  41.1 6.4 %copy-start.14 = (f32[4096,256]{1,0:T(8,128)S(1)}, f32[4096,256]{1,0:T(8,128)}, u32[]{:S(2)}) copy-start(f32[4096,256]{1,0:T(8,128)} %fusion.40) | copy-start | bytes 12582916
  41.1 6.4 %copy-start.24 = (bf16[2,256,256]{2,1,0:T(8,128)(2,1)S(1)}, bf16[2,256,256]{2,1,0:T(8,128)(2,1)}, u32[]{:S(2)}) copy-start(bf16[2,256,256]{2,1,0:T(8,128)(2,1)} %param.17) | copy-start | bytes 786436
  47.5 3.4 copy-start.16
  47.5 3.4 copy-start.4
  47.5 3.3 copy-start.27
  50.8 1.3 copy-start.18
  50.8 8.2 %copy-start.23 = (bf16[2,256,256]{2,1,0:T(8,128)(2,1)S(1)}, bf16[2,256,256]{2,1,0:T(8,128)(2,1)}, u32[]{:S(2)}) copy-start(bf16[2,256,256]{2,1,0:T(8,128)(2,1)} %param.16) | copy-start | bytes 786436
  53.3 15.9 %collective-permute-start.2 = (bf16[8,128,256]{2,1,0:T(8,128)(2,1)S(1)}, bf16[8,128,256]{2,1,0:T(8,128)(2,1)S(1)}, u32[]{:S(2)}, u32[]{:S(2)}) collective-permute-start(bf16[8,128,256]{2,1,0:T(8,128)(2,1)S(1)} %gather_fusion.3), channel_id=1, source_target_pairs={{0,1},{1,2},{2,3},{3,4},{4,5},{5,6},{6,7},{7,8},{8,9},{9,10},{10,1... | collective-permute-start | bytes 1572872 | tf_op jit(solution)/shard_map/ppermute | solution.py:10
  53.5 15.8 %collective-permute-start.3 = (bf16[8,128,256]{2,1,0:T(8,128)(2,1)S(1)}, bf16[8,128,256]{2,1,0:T(8,128)(2,1)S(1)}, u32[]{:S(2)}, u32[]{:S(2)}) collective-permute-start(bf16[8,128,256]{2,1,0:T(8,128)(2,1)S(1)} %gather_fusion.4), channel_id=1, source_target_pairs={{0,127},{1,0},{2,1},{3,2},{4,3},{5,4},{6,5},{7,6},{8,7},{9,8},{10,... | collective-permute-start | bytes 1572872 | tf_op jit(solution)/shard_map/ppermute | solution.py:10
  80.1 6.4 %copy-start.13 = (f32[4096,256]{1,0:T(8,128)S(1)}, f32[4096,256]{1,0:T(8,128)}, u32[]{:S(2)}) copy-start(f32[4096,256]{1,0:T(8,128)} %fusion.33) | copy-start | bytes 12582916
  80.1 6.4 %copy-start.25 = (bf16[2,256,256]{2,1,0:T(8,128)(2,1)S(1)}, bf16[2,256,256]{2,1,0:T(8,128)(2,1)}, u32[]{:S(2)}) copy-start(bf16[2,256,256]{2,1,0:T(8,128)(2,1)} %param.17) | copy-start | bytes 786436
  86.5 2.7 copy-start.21
  86.5 2.7 copy-start.28
  92.5 1.3 copy-start.11
  93.8 2.3 copy-start.1
  161.7 10.2 %copy-start.20 = (bf16[4096,256]{1,0:T(8,128)(2,1)S(1)}, bf16[4096,256]{1,0:T(8,128)(2,1)}, u32[]{:S(2)}) copy-start(bf16[4096,256]{1,0:T(8,128)(2,1)} %get-tuple-element.36) | copy-start | bytes 6291460
  165.1 10.5 %slice-start = ((s8[6291456]{0:T(1024)(128)(4,1)}), s8[4194304]{0:T(1024)(128)(4,1)S(1)}, s32[]{:S(2)}) async-start(s8[6291456]{0:T(1024)(128)(4,1)} %bitcast.145), calls=%async_computation.1 | async-start | bytes 8388608
  166.0 15.6 %collective-permute-start.4 = (bf16[8,128,256]{2,1,0:T(8,128)(2,1)S(1)}, bf16[8,128,256]{2,1,0:T(8,128)(2,1)S(1)}, u32[]{:S(2)}, u32[]{:S(2)}) collective-permute-start(bf16[8,128,256]{2,1,0:T(8,128)(2,1)S(1)} %get-tuple-element.29), channel_id=1, source_target_pairs={{0,127},{1,0},{2,1},{3,2},{4,3},{5,4},{6,5},{7,6},{8,7},{9,8},{10,... | collective-permute-start | bytes 1572872 | tf_op jit(solution)/shard_map/ppermute | solution.py:10
  171.7 13.2 %collective-permute-start.5 = (bf16[8,128,256]{2,1,0:T(8,128)(2,1)}, bf16[8,128,256]{2,1,0:T(8,128)(2,1)}, u32[]{:S(2)}, u32[]{:S(2)}) collective-permute-start(bf16[8,128,256]{2,1,0:T(8,128)(2,1)} %get-tuple-element.28), channel_id=1, source_target_pairs={{0,1},{1,2},{2,3},{3,4},{4,5},{5,6},{6,7},{7,8},{8,9},{9,10},{10,1... | collective-permute-start | bytes 1572872 | tf_op jit(solution)/shard_map/ppermute | solution.py:10
  171.9 2.0 copy-start.12
  171.9 3.7 slice-start.1
  175.6 2.4 copy-start.22
  189.4 4.6 %copy-start.29 = (bf16[2,256,256]{2,1,0:T(8,128)(2,1)S(1)}, bf16[2,256,256]{2,1,0:T(8,128)(2,1)}, u32[]{:S(2)}) copy-start(bf16[2,256,256]{2,1,0:T(8,128)(2,1)} %param.19) | copy-start | bytes 786436
  189.4 4.7 %copy-start.30 = (f32[4096,256]{1,0:T(8,128)S(1)}, f32[4096,256]{1,0:T(8,128)}, u32[]{:S(2)}) copy-start(f32[4096,256]{1,0:T(8,128)} %get-tuple-element.35) | copy-start | bytes 12582916
  194.0 3.5 copy-start.6
  194.1 3.4 copy-start.17
  197.5 2.2 copy-start.9
  197.5 1.5 copy-start.26
  199.0 2.2 copy-start.2
  267.0 10.1 %copy-start.5 = (bf16[4096,256]{1,0:T(8,128)(2,1)S(1)}, bf16[4096,256]{1,0:T(8,128)(2,1)}, u32[]{:S(2)}) copy-start(bf16[4096,256]{1,0:T(8,128)(2,1)} %param.10) | copy-start | bytes 6291460
  267.0 10.1 %copy-start.10 = (bf16[4096,256]{1,0:T(8,128)(2,1)S(1)}, bf16[4096,256]{1,0:T(8,128)(2,1)}, u32[]{:S(2)}) copy-start(bf16[4096,256]{1,0:T(8,128)(2,1)} %copy-done.9) | copy-start | bytes 6291460
  270.4 8.2 %copy-start = (f32[48,128,256]{2,1,0:T(8,128)S(1)}, f32[48,128,256]{2,1,0:T(8,128)}, u32[]{:S(2)}) copy-start(f32[48,128,256]{2,1,0:T(8,128)} %scatter_fusion.3) | copy-start | bytes 18874372
  271.3 83.2 %collective-permute-start.6 = (bf16[8,128,256]{2,1,0:T(8,128)(2,1)S(1)}, bf16[8,128,256]{2,1,0:T(8,128)(2,1)}, u32[]{:S(2)}, u32[]{:S(2)}) collective-permute-start(bf16[8,128,256]{2,1,0:T(8,128)(2,1)S(1)} %get-tuple-element.27), channel_id=1, source_target_pairs={{0,127},{1,0},{2,1},{3,2},{4,3},{5,4},{6,5},{7,6},{8,7},{9,8},{10,... | collective-permute-start | bytes 1572872 | tf_op jit(solution)/shard_map/ppermute | solution.py:10
  277.1 81.8 %collective-permute-start.7 = (bf16[8,128,256]{2,1,0:T(8,128)(2,1)}, bf16[8,128,256]{2,1,0:T(8,128)(2,1)}, u32[]{:S(2)}, u32[]{:S(2)}) collective-permute-start(bf16[8,128,256]{2,1,0:T(8,128)(2,1)} %get-tuple-element.26), channel_id=1, source_target_pairs={{0,1},{1,2},{2,3},{3,4},{4,5},{5,6},{6,7},{7,8},{8,9},{9,10},{10,1... | collective-permute-start | bytes 1572872 | tf_op jit(solution)/shard_map/ppermute | solution.py:10
  278.6 2.5 copy-start.7
  278.6 3.7 copy-start.19
  363.4 4.6 %copy-start.8 = (bf16[4096,256]{1,0:T(8,128)(2,1)S(1)}, bf16[4096,256]{1,0:T(8,128)(2,1)}, u32[]{:S(2)}) copy-start(bf16[4096,256]{1,0:T(8,128)(2,1)} %copy-done.6) | copy-start | bytes 6291460
  363.4 4.7 %copy-start.15 = (bf16[1,4096,256]{2,1,0:T(8,128)(2,1)S(1)}, bf16[1,4096,256]{2,1,0:T(8,128)(2,1)}, u32[]{:S(2)}) copy-start(bf16[1,4096,256]{2,1,0:T(8,128)(2,1)} %fusion.8) | copy-start | bytes 6291460
Sparse Core Ops, SparseCore 0:
  284.5 156.4 all-reduce.3
where the time goes:
time: 460 us; the launch traced here: 452 us
  other arithmetic  110 us (24%)
  waiting for transfers between devices  81.9 us (18%)
  local copies, waits for them, and re-layouts  80.1 us (17%)
  matrix products  71.7 us (16%)
  blocking collectives  69.5 us (15%)
  starting transfers between devices  23.6 us (5%)
  between operations  15.4 us (3%)
    scatter-add x2, other arithmetic, backward(): jax.ops.segment_sum(contrib.reshape(tile_count * slot_count, tile_rows, -...  73.5 us
    psum x1, blocking collectives, per_device(): lax.psum((early[0], early[1], early[2], early[3], later[0], later[1], lat...  69.5 us
    psum x1, waiting for transfers between devices, per_device(): lax.psum((early[0], early[1], early[2], early[3], later[0], later[1], lat...  69.3 us
    reshape x2, local copies, waits for them, and re-layouts, backward(): contrib.reshape(tile_count * slot_count, tile_rows, -1)  34.9 us
    ppermute x8, starting transfers between devices, passed_along(): return lax.ppermute(value, axis, pairs)  23.5 us
    gather x2, local copies, waits for them, and re-layouts, forward(): picked = extended[neighbours]  17 us
    dot_general x2, matrix products, backward(): jnp.einsum('tkij,tic->tkjc', adjacency, grad_gathered.reshape(tile_count,...  16.2 us
    dot_general x2, matrix products, forward(): jnp.einsum('tkij,tkjc->tic', adjacency, picked, preferred_element_type=jn...  12.7 us
  transfers between devices with their start and end apart: 9, of which 5 were waited for; matrix products, arithmetic and copies ran while one was open for 10% of the time, Pallas kernels for 0%

commit v1 on v0

v1 whole, which is shorter than its diff:
```python
import functools

import jax
import jax.numpy as jnp
from jax import lax
from jax.experimental import pallas as pl
from jax.experimental.pallas import tpu as pltpu
from jax.sharding import PartitionSpec as P

AXES = ("dom", "phase", "feat")
MESH = pl.DeviceIdType.MESH
BF = jnp.bfloat16
F32 = jnp.float32
NT = 32
LENT = 16
ROWS = 128
HID = 256
PAIRS = 96
GROUP = 48
GRADS = 1024


def dot(a, b):
    return lax.dot_general(a, b, (((1,), (0,)), ((), ())), preferred_element_type=F32)


def dot_rows(a, b):
    return lax.dot_general(a, b, (((0,), (0,)), ((), ())), preferred_element_type=F32)


def chip_id(x, y, core, z):
    return (x * 4 + (y // 2) * 2 + core, y % 2, z)


def part_id(part):
    return (part // 8, (part // 4) % 2, part % 4)


def build_tables(nbr_vec, bound_sm, tab_v):
    i32 = jnp.int32
    lane32 = lax.broadcasted_iota(i32, (NT, 128), 1)
    row32 = lax.broadcasted_iota(i32, (NT, 128), 0)
    spread = jnp.zeros((NT, 128), i32)
    for k in range(4):
        here = (lane32 // 4 == row32) & (lane32 % 4 == k)
        spread = spread + jnp.where(here, jnp.broadcast_to(nbr_vec[:, k : k + 1], (NT, 128)), 0)
    target = jnp.sum(spread, axis=0, keepdims=True)
    lane = lax.broadcasted_iota(i32, (1, 128), 1)
    key = jnp.where(lane % 4 == 0, 4096, jnp.where(lane // 4 < LENT, 256, 0) + target)
    li = lax.broadcasted_iota(i32, (128, 128), 1)
    ri = lax.broadcasted_iota(i32, (128, 128), 0)
    key_l = jnp.broadcast_to(key, (128, 128))
    key_c = jnp.sum(jnp.where(li == ri, key_l, 0), axis=1, keepdims=True)
    key_r = jnp.broadcast_to(key_c, (128, 128))
    before = (key_l < key_r) | ((key_l == key_r) & (li < ri))
    rank = jnp.sum(jnp.where(before, 1, 0), axis=1, keepdims=True)
    same = jnp.sum(jnp.where((key_l == key_r) & (li < ri), 1, 0), axis=1, keepdims=True)
    place = jnp.broadcast_to(rank, (128, 128)) == li
    order = jnp.sum(jnp.where(place, ri, 0), axis=0, keepdims=True)
    joins = jnp.sum(jnp.where(place, jnp.broadcast_to(same, (128, 128)), 0), axis=0, keepdims=True)
    slot = lane
    for q in range(LENT):
        slot = jnp.where(lane == bound_sm[0, q // 8, q % 8], q, slot)
    rows = [slot, order, joins]
    for base in (0, 256):
        upto = jnp.sum(jnp.where(key_r <= li + base, 1, 0), axis=0, keepdims=True) - 1
        rows.append(jnp.maximum(upto, 0))
        rows.append(jnp.sum(jnp.where(key_r == li + base, 1, 0), axis=0, keepdims=True))
    for n, row in enumerate(rows):
        tab_v[n : n + 1, :] = row


def mega(
    node_h, cot_h, adj_h, nbr_v, nbr_s, bound_s, live_s, wself_h, wnbr_h, bias_v, wout_h,
    out_h, grad_h, sums_h,
    adj, adj_t, cot, lent, ext0, ext1, agg0, agg1, act0, act1, slope0, dpre, dagg, scan, direct, mid,
    ret1, ret0, send1, send0, w_in, w_out, w_out_t, w_self_t, w_nbr_t,
    total, pack, rc, rx, ry, rz, full, tab_v, tab,
    load_sem, tab_sem, store_sem, hs, hr, gs, gr,
):
    dom, phase, feat = (lax.axis_index(a) for a in AXES)
    x, core = dom // 4, dom % 2
    y = ((dom // 2) % 2) * 2 + phase
    z = feat
    part = dom * 8 + phase * 4 + feat
    west = part_id((part + 127) % 128)
    east = part_id((part + 1) % 128)
    sides = (west, east)
    sibling = chip_id(x, y, 1 - core, z)
    x_ids = [chip_id((x + d) % 4, y, core, z) for d in (1, 2, 3)]
    y_ids = [chip_id(x, (y + d) % 4, core, z) for d in (1, 2, 3)]
    z_ids = [chip_id(x, y, core, (z + d) % 4) for d in (1, 2, 3)]

    loads = [
        pltpu.make_async_copy(node_h.at[pl.ds(0, LENT)], lent, load_sem.at[0]),
        pltpu.make_async_copy(node_h.at[pl.ds(LENT, LENT)], ext0.at[pl.ds(LENT, LENT)], load_sem.at[1]),
        pltpu.make_async_copy(adj_h, adj, load_sem.at[2]),
        pltpu.make_async_copy(wself_h.at[0], w_in.at[0, pl.ds(0, HID)], load_sem.at[3]),
        pltpu.make_async_copy(wself_h.at[1], w_in.at[1, pl.ds(0, HID)], load_sem.at[4]),
        pltpu.make_async_copy(wnbr_h.at[0], w_in.at[0, pl.ds(HID, HID)], load_sem.at[5]),
        pltpu.make_async_copy(wnbr_h.at[1], w_in.at[1, pl.ds(HID, HID)], load_sem.at[6]),
        pltpu.make_async_copy(wout_h, w_out, load_sem.at[7]),
        pltpu.make_async_copy(cot_h, cot, load_sem.at[8]),
    ]
    for copy in loads:
        copy.start()

    barrier = pltpu.get_barrier_semaphore()
    greeted = [west, east, sibling, *x_ids, *y_ids, *z_ids]
    for device in greeted:
        pl.semaphore_signal(barrier, inc=1, device_id=device, device_id_type=MESH)
    pl.semaphore_wait(barrier, len(greeted))

    def remote(src, dst, ssem, rsem, device):
        return pltpu.make_async_remote_copy(
            src_ref=src, dst_ref=dst, send_sem=ssem, recv_sem=rsem, device_id=device, device_id_type=MESH
        )

    def halo(n, src, dst, side, j):
        place = 40 + j if side == 0 else 32 + j
        return remote(src.at[side * 8 + j], dst.at[place], hs.at[n, side, j], hr.at[n, side, j], sides[side])

    def back(n, src, dst, side, j):
        place = 8 + j if side == 0 else j
        return remote(src.at[side * 8 + j], dst.at[place], hs.at[n, side, j], hr.at[n, side, j], sides[side])

    loads[0].wait()

    def give(j, c):
        for side in (0, 1):
            ext0[side * 8 + j] = lent[bound_s[0, side, j]]
            halo(0, ext0, ext0, side, j).start()
        return c

    lax.fori_loop(0, 8, give, 0)

    build_tables(nbr_v[...], bound_s, tab_v)
    tab_copy = pltpu.make_async_copy(tab_v, tab, tab_sem)
    tab_copy.start()
    for copy in loads[1:]:
        copy.wait()
    for s in (0, 1):
        w_out_t[s] = w_out[s].T
        w_self_t[s] = w_in[s, 0:HID].T
        w_nbr_t[s] = w_in[s, HID : 2 * HID].T
        total[s] = jnp.zeros((GRADS, HID), F32)

    def flip(t, c):
        for k in range(4):
            adj_t[t * 4 + k] = adj[t, k].T
        return c

    lax.fori_loop(0, NT, flip, 0)
    tab_copy.wait()
    live = live_s[0]

    def alive(q):
        return jnp.where(q < live, 1.0, 0.0).astype(F32)

    def cot_of(t, masked):
        c = cot[t]
        return (c.astype(F32) * alive(t)).astype(BF) if masked else c

    def tiles_of(group, i, count):
        if group:
            return [(LENT + i * count + n, LENT + i * count + n) for n in range(count)]
        half = count // 2
        return [
            (bound_s[0, side, i * half + n], side * 8 + i * half + n) for n in range(half) for side in (0, 1)
        ]

    def stacked(ref, tiles):
        return jnp.concatenate([ref[q] for _, q in tiles], axis=0)

    def put(ref, tiles, value):
        for n, (_, q) in enumerate(tiles):
            ref[q] = value[n * ROWS : (n + 1) * ROWS]

    def slope_up(group, i, c):
        tiles = tiles_of(group, i, 4)
        m = jnp.concatenate([cot_of(t, group) for t, _ in tiles], axis=0)
        put(scan, tiles, dot(m, w_out_t[1]))
        return c

    lax.fori_loop(0, 4, functools.partial(slope_up, 0), 0)
    lax.fori_loop(0, 4, functools.partial(slope_up, 1), 0)

    def gathered(ext, tiles):
        parts = []
        for t, _ in tiles:
            left = jnp.concatenate([adj[t, k] for k in range(4)], axis=1)
            right = jnp.concatenate([ext[tab[0, nbr_s[t, k]]] for k in range(4)], axis=0)
            parts.append(dot(left, right).astype(BF))
        return jnp.concatenate(parts, axis=0)

    def layer(s, ext, agg, act, tiles):
        f = stacked(ext, tiles)
        a = gathered(ext, tiles)
        put(agg, tiles, a)
        pre = dot(jnp.concatenate([f, a], axis=1), w_in[s]) + bias_v[s : s + 1, :]
        gate = 0.5 * jnp.tanh(0.5 * pre) + 0.5
        hidden = pre * gate
        h = hidden.astype(BF)
        put(act, tiles, h)
        return f, h, gate + hidden * (1.0 - gate)

    def masked_rows(group, tiles, value):
        if not group:
            return value
        return jnp.concatenate(
            [value[n * ROWS : (n + 1) * ROWS] * alive(t) for n, (t, _) in enumerate(tiles)], axis=0
        )

    def first(group, i, c):
        tiles = tiles_of(group, i, 2)
        f, h, slope = layer(0, ext0, agg0, act0, tiles)
        put(slope0, tiles, slope)
        out = masked_rows(group, tiles, f.astype(F32) + dot(h, w_out[0])).astype(BF)
        put(ext1, tiles, out)
        if not group:
            for side in (0, 1):
                halo(1, ext1, ext1, side, i).start()
        return c

    def land(n, ext, j, c):
        for side in (0, 1):
            halo(n, ext, ext, side, j).wait_recv()
        return c

    lax.fori_loop(0, 8, functools.partial(land, 0, ext0), 0)
    lax.fori_loop(0, 8, functools.partial(first, 0), 0)
    lax.fori_loop(0, 8, functools.partial(first, 1), 0)

    lax.fori_loop(0, 8, functools.partial(land, 1, ext1), 0)

    def second(group, i, c):
        tiles = tiles_of(group, i, 4)
        _, _, slope = layer(1, ext1, agg1, act1, tiles)
        d = (stacked(scan, tiles) * slope).astype(BF)
        put(dpre, tiles, d)
        put(dagg, tiles, dot(d, w_nbr_t[1]).astype(BF))
        return c

    lax.fori_loop(0, 4, functools.partial(second, 0), 0)
    lax.fori_loop(0, 4, functools.partial(second, 1), 0)

    def pair(r, c):
        i = tab[1, r]
        value = dot(adj_t[i], dagg[tab[0, i // 4]])
        earlier = scan[jnp.maximum(r - 1, 0)]
        scan[r] = value + jnp.where(tab[2, r] > 0, earlier, jnp.zeros_like(earlier))
        return c

    def pairs(begin, end):
        lax.fori_loop(begin, end, pair, 0)

    def collected(target):
        low = scan[tab[3, target]]
        high = scan[tab[5, target]]
        nil = jnp.zeros_like(low)
        return jnp.where(tab[4, target] > 0, low, nil) + jnp.where(tab[6, target] > 0, high, nil)

    def give_back(n, src, dst, j, c):
        for side in (0, 1):
            src[side * 8 + j] = collected(32 + side * 8 + j).astype(BF)
            back(n, src, dst, side, j).start()
        return c

    pairs(0, GROUP)
    pairs(GROUP, PAIRS)
    lax.fori_loop(0, 8, functools.partial(give_back, 2, send1, ret1), 0)

    def unlent(src, dst, t, c):
        dst[t] = src[tab[0, t]]
        return c

    lax.fori_loop(0, LENT, functools.partial(unlent, ext1, send0), 0)
    store_a = pltpu.make_async_copy(send0, out_h.at[0, pl.ds(0, LENT)], store_sem.at[0])
    store_b = pltpu.make_async_copy(ext1.at[pl.ds(LENT, LENT)], out_h.at[0, pl.ds(LENT, LENT)], store_sem.at[1])
    store_a.start()
    store_b.start()

    def straight(s, tiles, m):
        d = dot(stacked(dpre, tiles), w_self_t[s])
        parts = []
        for n, (t, q) in enumerate(tiles):
            own = dot(adj_t[t * 4], dagg[q]) + collected(t)
            parts.append(m[n * ROWS : (n + 1) * ROWS].astype(F32) + d[n * ROWS : (n + 1) * ROWS] + own)
        return jnp.concatenate(parts, axis=0)

    def add_grads(s, ext, agg, act, tiles, m):
        d = stacked(dpre, tiles)
        total[s, 0:HID] += dot_rows(stacked(ext, tiles), d)
        total[s, HID : 2 * HID] += dot_rows(stacked(agg, tiles), d)
        total[s, 2 * HID : 3 * HID] += dot_rows(stacked(act, tiles), m)
        total[s, 3 * HID : 3 * HID + 1] += jnp.sum(d.astype(F32), axis=0, keepdims=True)

    def later(group, i, c):
        tiles = tiles_of(group, i, 4)
        m = jnp.concatenate([cot_of(t, group) for t, _ in tiles], axis=0)
        add_grads(1, ext1, agg1, act1, tiles, m)
        value = straight(1, tiles, m)
        if group:
            put(mid, tiles, value.astype(BF))
        else:
            put(direct, tiles, value)
        return c

    lax.fori_loop(0, 4, functools.partial(later, 0), 0)
    lax.fori_loop(0, 4, functools.partial(later, 1), 0)

    def core_step(s):
        return remote(pack.at[s, pl.ds((1 - core) * 512, 512)], rc.at[s], gs.at[s, 0, 0], gr.at[s, 0, 0], sibling)

    def x_step(s, d):
        rows = pl.ds(core * 512 + ((x + d) % 4) * 128, 128)
        return remote(pack.at[s, rows], rx.at[s, d - 1], gs.at[s, 1, d - 1], gr.at[s, 1, d - 1], x_ids[d - 1])

    def y_step(s, d):
        rows = pl.ds(core * 512 + x * 128 + ((y + d) % 4) * 32, 32)
        return remote(pack.at[s, rows], ry.at[s, d - 1], gs.at[s, 2, d - 1], gr.at[s, 2, d - 1], y_ids[d - 1])

    def z_step(s, d):
        return remote(rz.at[s, z], rz.at[s, z], gs.at[s, 3, d - 1], gr.at[s, 3, d - 1], z_ids[d - 1])

    def spread_step(s, level, d):
        base, size = (
            (core * 512 + x * 128 + y * 32, 32),
            (core * 512 + x * 128, 128),
            (core * 512, 512),
        )[level]
        rows = full.at[s, pl.ds(base, size)]
        device = (y_ids, x_ids, [sibling])[level][d - 1]
        return remote(rows, rows, gs.at[s, 4 + level, d - 1], gr.at[s, 4 + level, d - 1], device)

    def sums_begin(s):
        other = pl.ds((1 - core) * 512, 512)
        pack[s, other] = total[s, other].astype(BF)
        core_step(s).start()

    def sums_x(s):
        core_step(s).wait_recv()
        own = pl.ds(core * 512, 512)
        value = total[s, own] + rc[s].astype(F32)
        total[s, own] = value
        pack[s, own] = value.astype(BF)
        for d in (1, 2, 3):
            x_step(s, d).start()

    def sums_y(s):
        for d in (1, 2, 3):
            x_step(s, d).wait()
        own = pl.ds(core * 512 + x * 128, 128)
        value = total[s, own] + rx[s, 0].astype(F32) + rx[s, 1].astype(F32) + rx[s, 2].astype(F32)
        total[s, own] = value
        pack[s, own] = value.astype(BF)
        for d in (1, 2, 3):
            y_step(s, d).start()

    def sums_z(s):
        for d in (1, 2, 3):
            y_step(s, d).wait_recv()
        own = pl.ds(core * 512 + x * 128 + y * 32, 32)
        value = total[s, own] + ry[s, 0].astype(F32) + ry[s, 1].astype(F32) + ry[s, 2].astype(F32)
        rz[s, z] = value.astype(BF)
        for d in (1, 2, 3):
            z_step(s, d).start()

    def z_landed(s, d):
        src = rz.at[s, (z + 4 - d) % 4]
        return remote(src, src, gs.at[s, 3, d - 1], gr.at[s, 3, d - 1], z_ids[d - 1])

    def sums_back(s):
        for d in (1, 2, 3):
            z_landed(s, d).wait_recv()
        value = rz[s, 0].astype(F32) + rz[s, 1].astype(F32) + rz[s, 2].astype(F32) + rz[s, 3].astype(F32)
        full[s, pl.ds(core * 512 + x * 128 + y * 32, 32)] = value.astype(BF)
        for d in (1, 2, 3):
            spread_step(s, 0, d).start()

    def landed(s, level, d):
        base, size = (
            (core * 512 + x * 128 + ((y + 4 - d) % 4) * 32, 32),
            (core * 512 + ((x + 4 - d) % 4) * 128, 128),
            ((1 - core) * 512, 512),
        )[level]
        rows = full.at[s, pl.ds(base, size)]
        return remote(rows, rows, gs.at[s, 4 + level, d - 1], gr.at[s, 4 + level, d - 1], sibling)

    def sums_up(s, level):
        for d in (1, 2, 3):
            landed(s, level, d).wait_recv()
        for d in (1, 2, 3) if level == 0 else (1,):
            spread_step(s, level + 1, d).start()

    def sums_end(s):
        landed(s, 2, 1).wait_recv()
        store = pltpu.make_async_copy(full.at[s], sums_h.at[s], store_sem.at[6 + s])
        store.start()
        return store

    sums_begin(1)

    def last_out(i, c):
        ts = [i * 4 + n for n in range(4)]
        qs = [tab[0, t] for t in ts]
        h = jnp.concatenate([act1[q] for q in qs], axis=0)
        f = jnp.concatenate([ext1[q] for q in qs], axis=0)
        value = f.astype(F32) + dot(h, w_out[1])
        for n, t in enumerate(ts):
            cot[t] = (value[n * ROWS : (n + 1) * ROWS] * alive(t)).astype(BF)
        return c

    def pull(tiles, m):
        d = (dot(m, w_out_t[0]) * stacked(slope0, tiles)).astype(BF)
        put(dpre, tiles, d)
        put(dagg, tiles, dot(d, w_nbr_t[0]).astype(BF))

    def early_rest(i, c):
        tiles = tiles_of(1, i, 4)
        m = jnp.concatenate([(mid[q].astype(F32) * alive(t)).astype(BF) for t, q in tiles], axis=0)
        pull(tiles, m)
        add_grads(0, ext0, agg0, act0, tiles, m)
        return c

    lax.fori_loop(0, 4, early_rest, 0)
    pairs(0, GROUP)
    sums_x(1)
    lax.fori_loop(0, 8, last_out, 0)
    store_c = pltpu.make_async_copy(cot, out_h.at[1], store_sem.at[2])
    store_c.start()
    store_d = pltpu.make_async_copy(mid.at[pl.ds(LENT, LENT)], grad_h.at[1, pl.ds(LENT, LENT)], store_sem.at[3])
    store_d.start()
    sums_y(1)

    def early(i, c):
        for side in (0, 1):
            back(2, send1, ret1, side, i).wait_recv()
        tiles = tiles_of(0, i, 2)
        m = (stacked(direct, tiles) + stacked(ret1, tiles).astype(F32)).astype(BF)
        put(mid, tiles, m)
        pull(tiles, m)
        add_grads(0, ext0, agg0, act0, tiles, m)
        return c

    lax.fori_loop(0, 8, early, 0)
    sums_begin(0)
    sums_z(1)
    store_a.wait()
    pairs(GROUP, PAIRS)
    lax.fori_loop(0, 8, functools.partial(give_back, 3, send0, ret0), 0)
    sums_x(0)
    sums_back(1)

    lax.fori_loop(0, LENT, functools.partial(unlent, mid, lent), 0)
    store_e = pltpu.make_async_copy(lent, grad_h.at[1, pl.ds(0, LENT)], store_sem.at[4])
    store_e.start()

    def whole(group, i, c):
        tiles = tiles_of(group, i, 4)
        if group:
            m = jnp.concatenate([(mid[q].astype(F32) * alive(t)).astype(BF) for t, q in tiles], axis=0)
            put(act1, tiles, straight(0, tiles, m).astype(BF))
        else:
            put(direct, tiles, straight(0, tiles, stacked(mid, tiles)))
        return c

    lax.fori_loop(0, 4, functools.partial(whole, 1), 0)
    sums_y(0)
    sums_up(1, 0)
    lax.fori_loop(0, 4, functools.partial(whole, 0), 0)
    store_f = pltpu.make_async_copy(act1.at[pl.ds(LENT, LENT)], grad_h.at[0, pl.ds(LENT, LENT)], store_sem.at[5])
    store_f.start()
    sums_z(0)
    sums_up(1, 1)

    def arrive(j, c):
        for side in (0, 1):
            back(3, send0, ret0, side, j).wait_recv()
        return c

    lax.fori_loop(0, 8, arrive, 0)
    sums_back(0)

    def finish(t, c):
        q = tab[0, t]
        act1[t] = (direct[q] + ret0[q].astype(F32)).astype(BF)
        return c

    lax.fori_loop(0, LENT, finish, 0)
    store_g = pltpu.make_async_copy(act1.at[pl.ds(0, LENT)], grad_h.at[0, pl.ds(0, LENT)], store_sem.at[0])
    store_g.start()
    store_h = sums_end(1)
    sums_up(0, 0)
    sums_up(0, 1)
    store_i = sums_end(0)

    def drain(j, c):
        for side in (0, 1):
            halo(0, ext0, ext0, side, j).wait_send()
            halo(1, ext1, ext1, side, j).wait_send()
            back(2, send1, ret1, side, j).wait_send()
            back(3, send0, ret0, side, j).wait_send()
        return c

    lax.fori_loop(0, 8, drain, 0)
    for s in (1, 0):
        core_step(s).wait_send()
        for d in (1, 2, 3):
            y_step(s, d).wait_send()
            z_step(s, d).wait_send()
            spread_step(s, 0, d).wait_send()
            spread_step(s, 1, d).wait_send()
        spread_step(s, 2, 1).wait_send()
    for copy in (store_b, store_c, store_d, store_e, store_f, store_g, store_h, store_i):
        copy.wait()


def per_device(
    node_in, out_cot, adjacency, tile_nbrs, bound_tiles, live_tiles, w_self, w_nbr, pre_bias, w_out
):
    anyspace = pl.BlockSpec(memory_space=pl.ANY)
    vmem = pl.BlockSpec(memory_space=pltpu.VMEM)
    smem = pl.BlockSpec(memory_space=pltpu.SMEM)
    tiles = lambda n, dtype=BF: pltpu.VMEM((n, ROWS, HID), dtype)
    dma = pltpu.SemaphoreType.DMA
    scratch = [
        pltpu.VMEM((NT, 4, ROWS, ROWS), BF),
        pltpu.VMEM((NT * 4, ROWS, ROWS), BF),
        tiles(NT),
        tiles(LENT),
        tiles(48),
        tiles(48),
        tiles(NT),
        tiles(NT),
        tiles(NT),
        tiles(NT),
        tiles(NT, F32),
        tiles(NT),
        tiles(NT),
        tiles(PAIRS, F32),
        tiles(LENT, F32),
        tiles(NT),
        tiles(LENT),
        tiles(LENT),
        tiles(LENT),
        tiles(LENT),
        pltpu.VMEM((2, 2 * HID, HID), BF),
        pltpu.VMEM((2, HID, HID), BF),
        pltpu.VMEM((2, HID, HID), BF),
        pltpu.VMEM((2, HID, HID), BF),
        pltpu.VMEM((2, HID, HID), BF),
        pltpu.VMEM((2, GRADS, HID), F32),
        pltpu.VMEM((2, GRADS, HID), BF),
        pltpu.VMEM((2, 512, HID), BF),
        pltpu.VMEM((2, 3, 128, HID), BF),
        pltpu.VMEM((2, 3, 32, HID), BF),
        pltpu.VMEM((2, 4, 32, HID), BF),
        pltpu.VMEM((2, GRADS, HID), BF),
        pltpu.VMEM((8, 128), jnp.int32),
        pltpu.SMEM((8, 128), jnp.int32),
        dma((9,)),
        dma,
        dma((8,)),
        dma((4, 2, 8)),
        dma((4, 2, 8)),
        dma((2, 7, 3)),
        dma((2, 7, 3)),
    ]
    out, grad, sums = pl.pallas_call(
        mega,
        out_shape=(
            jax.ShapeDtypeStruct((2, NT, ROWS, HID), BF),
            jax.ShapeDtypeStruct((2, NT, ROWS, HID), BF),
            jax.ShapeDtypeStruct((2, GRADS, HID), BF),
        ),
        in_specs=[
            anyspace, anyspace, anyspace, vmem, smem, smem, smem, anyspace, anyspace, vmem, anyspace,
        ],
        out_specs=(anyspace, anyspace, anyspace),
        scratch_shapes=scratch,
        compiler_params=pltpu.CompilerParams(
            collective_id=0, has_side_effects=True, vmem_limit_bytes=67043328
        ),
        name="mesh_layers",
    )(
        node_in.reshape(NT, ROWS, HID), out_cot.reshape(NT, ROWS, HID), adjacency,
        tile_nbrs, tile_nbrs, bound_tiles, live_tiles, w_self, w_nbr, pre_bias, w_out,
    )
    rows = NT * ROWS
    grad_sums = sums.astype(F32)
    return (
        out.reshape(2, rows, HID),
        grad.reshape(2, rows, HID),
        grad_sums[:, 0:HID],
        grad_sums[:, HID : 2 * HID],
        grad_sums[:, 3 * HID],
        grad_sums[:, 2 * HID : 3 * HID],
    )


def solution(mesh):
    split = P(AXES)
    in_specs = (split,) * 6 + (P(),) * 4
    out_specs = (P(None, AXES), P(None, AXES), P(), P(), P(), P())
    return jax.shard_map(
        per_device, mesh=mesh, in_specs=in_specs, out_specs=out_specs, check_vma=False
    )
```

time: 460 us -> 135 us (0.29); the launches traced: 452 us -> 134 us
  Pallas kernels: 0 us -> 122 us
  other arithmetic: 110 us -> 0 us
  waiting for transfers between devices: 81.9 us -> 0 us
  matrix products: 71.7 us -> 0 us
  blocking collectives: 69.5 us -> 0 us
  local copies, waits for them, and re-layouts: 80.1 us -> 11.6 us
  starting transfers between devices: 23.6 us -> 0 us
  between operations: 15.4 us -> 1.29 us
    pallas_call x0 -> x1, Pallas kernels: none -> 122 us  [per_device(): pl.pallas_call(mega, out_shape=(jax.ShapeDtypeStruct((2, NT, ROWS, HID),...]
    scatter-add x6 -> x0, other arithmetic: 86.8 us -> none  [the longest x2 73.5 us: backward(): jax.ops.segment_sum(contrib.reshape(tile_count * slot_count, tile_rows, -...]
    dot_general x22 -> x0, matrix products: 71.7 us -> none  [the longest x2 16.2 us: backward(): jnp.einsum('tkij,tic->tkjc', adjacency, grad_gathered.reshape(tile_count,...]
    psum x1 -> x0, blocking collectives: 69.5 us -> none  [per_device(): lax.psum((early[0], early[1], early[2], early[3], later[0], later[1], lat...]
    psum x1 -> x0, waiting for transfers between devices: 69.3 us -> none  [per_device(): lax.psum((early[0], early[1], early[2], early[3], later[0], later[1], lat...]
    reshape x2 -> x0, local copies, waits for them, and re-layouts: 34.9 us -> none  [backward(): contrib.reshape(tile_count * slot_count, tile_rows, -1)]
    gather x6 -> x0, local copies, waits for them, and re-layouts: 24.1 us -> none  [the longest x2 17 us: forward(): picked = extended[neighbours]]
    ppermute x8 -> x0, starting transfers between devices: 23.5 us -> none  [passed_along(): return lax.ppermute(value, axis, pairs)]
  transfers between devices with their start and end apart: 9 -> 0, of which waited for: 5 -> 0; matrix products, arithmetic and copies ran while one was open for 10% -> 0% of each run, Pallas kernels for 0% -> 0%
where the time goes in v1:
time: 135 us; the launch traced here: 134 us
  Pallas kernels  122 us (90%)
  local copies, waits for them, and re-layouts  11.6 us (9%)
    pallas_call x1, Pallas kernels, per_device(): pl.pallas_call(mega, out_shape=(jax.ShapeDtypeStruct((2, NT, ROWS, HID),...  122 us
    unnamed x6, local copies, waits for them, and re-layouts  8.58 us

profile of v1, /device:TPU:1, one launch (start us, length us, event | category | flops | bytes accessed | tf_op | source)
XLA Modules:
  0.0 134.5 jit_solution(1151174799741542292)
XLA Ops:
  1.3 1.4 %copy.16.nbr_v.nbr_s = s32[32,4]{1,0:T(8,128)} copy(s32[32,4]{0,1:T(4,128)} %param.13) | data formatting | bytes 1024 | tf_op args[3]
  2.6 121.6 %mesh_layers.1 = (bf16[2,32,128,256]{3,2,1,0:T(8,128)(2,1)}, bf16[2,32,128,256]{3,2,1,0:T(8,128)(2,1)}, bf16[2,1024,256]{2,1,0:T(8,128)(2,1)}) custom-call(bf16[32,128,256]{2,1,0:T(8,128)(2,1)} %bitcast.9, bf16[32,128,256]{2,1,0:T(8,128)(2,1)} %bitcast.10, bf16[32,4,128,128]{3,2,1,0:T(8,128)(2,1)} %adj_h.1, s32[32,4]{1,0:T(8,128)} %copy.16.nbr_v.nbr_s, ...), custom_call_target="tpu_custom_call" | custom-call | tf_op jit(solution)/shard_map/mesh_layers/pallas_call | solution.py:570
  124.3 0.7 slice.18
  125.0 0.6 copy.20
  125.5 2.3 %fusion = (f32[2,256,256]{2,1,0:T(8,128)}, f32[2,256,256]{2,1,0:T(8,128)}, f32[2,256,256]{2,1,0:T(8,128)}) fusion(bf16[2,1024,256]{2,1,0:T(8,128)(2,1)} %get-tuple-element.11), kind=kLoop, calls=%fused_computation.1 | loop fusion | bytes 3145728 | tf_op jit(solution)/shard_map/slice | solution.py:598
  127.8 0.0 copy-start
  127.8 4.6 %copy.24 = bf16[2,4096,256]{2,1,0:T(8,128)(2,1)} copy(bf16[2,4096,256]{2,1,0:T(8,128)(2,1)} %bitcast.8) | data formatting | bytes 8388608
  132.4 0.0 copy-done
  132.4 2.0 %copy.25 = bf16[2,4096,256]{2,1,0:T(8,128)(2,1)} copy(bf16[2,4096,256]{2,1,0:T(8,128)(2,1)S(1)} %bitcast.7) | data formatting | bytes 8388608
Async XLA Ops:
  127.8 4.6 %copy-start = (bf16[2,32,128,256]{3,2,1,0:T(8,128)(2,1)S(1)}, bf16[2,32,128,256]{3,2,1,0:T(8,128)(2,1)}, u32[]{:S(2)}) copy-start(bf16[2,32,128,256]{3,2,1,0:T(8,128)(2,1)} %get-tuple-element.10) | copy-start | bytes 12582916

commit v2 on v1

--- a/solution.py
+++ b/solution.py
@@ -18,6 +18,8 @@
 PAIRS = 96
 GROUP = 48
 GRADS = 1024
+UNROLL = 8
+AHEAD = 2
 
 
 def dot(a, b):
@@ -40,10 +42,13 @@
     i32 = jnp.int32
     lane32 = lax.broadcasted_iota(i32, (NT, 128), 1)
     row32 = lax.broadcasted_iota(i32, (NT, 128), 0)
+    square = lax.broadcasted_iota(i32, (NT, NT), 0) == lax.broadcasted_iota(i32, (NT, NT), 1)
     spread = jnp.zeros((NT, 128), i32)
     for k in range(4):
+        line = jnp.broadcast_to(nbr_vec[k : k + 1, :], (NT, NT))
+        column = jnp.sum(jnp.where(square, line, 0), axis=1, keepdims=True)
         here = (lane32 // 4 == row32) & (lane32 % 4 == k)
-        spread = spread + jnp.where(here, jnp.broadcast_to(nbr_vec[:, k : k + 1], (NT, 128)), 0)
+        spread = spread + jnp.where(here, jnp.broadcast_to(column, (NT, 128)), 0)
     target = jnp.sum(spread, axis=0, keepdims=True)
     lane = lax.broadcasted_iota(i32, (1, 128), 1)
     key = jnp.where(lane % 4 == 0, 4096, jnp.where(lane // 4 < LENT, 256, 0) + target)
@@ -145,12 +150,6 @@
         w_nbr_t[s] = w_in[s, HID : 2 * HID].T
         total[s] = jnp.zeros((GRADS, HID), F32)
 
-    def flip(t, c):
-        for k in range(4):
-            adj_t[t * 4 + k] = adj[t, k].T
-        return c
-
-    lax.fori_loop(0, NT, flip, 0)
     tab_copy.wait()
     live = live_s[0]
 
@@ -182,14 +181,11 @@
         put(scan, tiles, dot(m, w_out_t[1]))
         return c
 
-    lax.fori_loop(0, 4, functools.partial(slope_up, 0), 0)
-    lax.fori_loop(0, 4, functools.partial(slope_up, 1), 0)
-
     def gathered(ext, tiles):
         parts = []
         for t, _ in tiles:
             left = jnp.concatenate([adj[t, k] for k in range(4)], axis=1)
-            right = jnp.concatenate([ext[tab[0, nbr_s[t, k]]] for k in range(4)], axis=0)
+            right = jnp.concatenate([ext[tab[0, nbr_s[k, t]]] for k in range(4)], axis=0)
             parts.append(dot(left, right).astype(BF))
         return jnp.concatenate(parts, axis=0)
 
@@ -230,6 +226,15 @@
     lax.fori_loop(0, 8, functools.partial(land, 0, ext0), 0)
     lax.fori_loop(0, 8, functools.partial(first, 0), 0)
     lax.fori_loop(0, 8, functools.partial(first, 1), 0)
+    lax.fori_loop(0, 4, functools.partial(slope_up, 0), 0)
+    lax.fori_loop(0, 4, functools.partial(slope_up, 1), 0)
+
+    def flip(t, c):
+        for k in range(4):
+            adj_t[t * 4 + k] = adj[t, k].T
+        return c
+
+    lax.fori_loop(0, NT, flip, 0)
 
     lax.fori_loop(0, 8, functools.partial(land, 1, ext1), 0)
 
@@ -244,15 +249,19 @@
     lax.fori_loop(0, 4, functools.partial(second, 0), 0)
     lax.fori_loop(0, 4, functools.partial(second, 1), 0)
 
-    def pair(r, c):
-        i = tab[1, r]
-        value = dot(adj_t[i], dagg[tab[0, i // 4]])
-        earlier = scan[jnp.maximum(r - 1, 0)]
-        scan[r] = value + jnp.where(tab[2, r] > 0, earlier, jnp.zeros_like(earlier))
+    def pair(base, i, c):
+        begin = base + i * UNROLL
+        total_so_far = scan[jnp.maximum(begin - 1, 0)]
+        for n in range(UNROLL):
+            p = tab[1, begin + n]
+            value = dot(adj_t[p], dagg[tab[0, p // 4]])
+            keep = tab[2, begin + n] > 0
+            total_so_far = value + jnp.where(keep, total_so_far, jnp.zeros_like(value))
+            scan[begin + n] = total_so_far
         return c
 
     def pairs(begin, end):
-        lax.fori_loop(begin, end, pair, 0)
+        lax.fori_loop(0, (end - begin) // UNROLL, functools.partial(pair, begin), 0)
 
     def collected(target):
         low = scan[tab[3, target]]
@@ -295,10 +304,15 @@
         total[s, 2 * HID : 3 * HID] += dot_rows(stacked(act, tiles), m)
         total[s, 3 * HID : 3 * HID + 1] += jnp.sum(d.astype(F32), axis=0, keepdims=True)
 
+    def later_grads(group, i, c):
+        tiles = tiles_of(group, i, 4)
+        m = jnp.concatenate([cot_of(t, group) for t, _ in tiles], axis=0)
+        add_grads(1, ext1, agg1, act1, tiles, m)
+        return c
+
     def later(group, i, c):
         tiles = tiles_of(group, i, 4)
         m = jnp.concatenate([cot_of(t, group) for t, _ in tiles], axis=0)
-        add_grads(1, ext1, agg1, act1, tiles, m)
         value = straight(1, tiles, m)
         if group:
             put(mid, tiles, value.astype(BF))
@@ -306,32 +320,43 @@
             put(direct, tiles, value)
         return c
 
-    lax.fori_loop(0, 4, functools.partial(later, 0), 0)
-    lax.fori_loop(0, 4, functools.partial(later, 1), 0)
-
     def core_step(s):
-        return remote(pack.at[s, pl.ds((1 - core) * 512, 512)], rc.at[s], gs.at[s, 0, 0], gr.at[s, 0, 0], sibling)
-
-    def x_step(s, d):
-        rows = pl.ds(core * 512 + ((x + d) % 4) * 128, 128)
-        return remote(pack.at[s, rows], rx.at[s, d - 1], gs.at[s, 1, d - 1], gr.at[s, 1, d - 1], x_ids[d - 1])
-
-    def y_step(s, d):
-        rows = pl.ds(core * 512 + x * 128 + ((y + d) % 4) * 32, 32)
-        return remote(pack.at[s, rows], ry.at[s, d - 1], gs.at[s, 2, d - 1], gr.at[s, 2, d - 1], y_ids[d - 1])
-
-    def z_step(s, d):
-        return remote(rz.at[s, z], rz.at[s, z], gs.at[s, 3, d - 1], gr.at[s, 3, d - 1], z_ids[d - 1])
-
-    def spread_step(s, level, d):
-        base, size = (
-            (core * 512 + x * 128 + y * 32, 32),
-            (core * 512 + x * 128, 128),
-            (core * 512, 512),
-        )[level]
-        rows = full.at[s, pl.ds(base, size)]
-        device = (y_ids, x_ids, [sibling])[level][d - 1]
-        return remote(rows, rows, gs.at[s, 4 + level, d - 1], gr.at[s, 4 + level, d - 1], device)
+        return remote(pack.at[s, pl.ds((1 - core) * 512, 512)], rc.at[s], gs.at[s, 0, 0, 0], gr.at[s, 0, 0, 0], sibling)
+
+    def order_of(h):
+        return ((x, x_ids), (y, y_ids)) if h == 0 else ((y, y_ids), (x, x_ids))
+
+    def columns(h):
+        return pl.ds(h * 128, 128)
+
+    def one_step(s, h, d):
+        (p, ids), _ = order_of(h)
+        rows = pl.ds(core * 512 + ((p + d) % 4) * 128, 128)
+        src = pack.at[s, rows, columns(h)]
+        return remote(src, rx.at[s, h, d - 1], gs.at[s, h, 1, d - 1], gr.at[s, h, 1, d - 1], ids[d - 1])
+
+    def two_step(s, h, d):
+        (p, _), (q, ids) = order_of(h)
+        rows = pl.ds(core * 512 + p * 128 + ((q + d) % 4) * 32, 32)
+        src = pack.at[s, rows, columns(h)]
+        return remote(src, ry.at[s, h, d - 1], gs.at[s, h, 2, d - 1], gr.at[s, h, 2, d - 1], ids[d - 1])
+
+    def z_step(s, d, slot):
+        here = rz.at[s, slot]
+        return remote(here, here, gs.at[s, 0, 3, d - 1], gr.at[s, 0, 3, d - 1], z_ids[d - 1])
+
+    def spread_step(s, h, level, d, back_by=0):
+        (p, ids_p), (q, ids_q) = order_of(h)
+        if level == 0:
+            base, size, ids = core * 512 + p * 128 + ((q + 4 - back_by) % 4) * 32, 32, ids_q
+        else:
+            base, size, ids = core * 512 + ((p + 4 - back_by) % 4) * 128, 128, ids_p
+        rows = full.at[s, pl.ds(base, size), columns(h)]
+        return remote(rows, rows, gs.at[s, h, 4 + level, d - 1], gr.at[s, h, 4 + level, d - 1], ids[d - 1])
+
+    def half_step(s, half):
+        rows = full.at[s, pl.ds(half * 512, 512)]
+        return remote(rows, rows, gs.at[s, 0, 6, 0], gr.at[s, 0, 6, 0], sibling)
 
     def sums_begin(s):
         other = pl.ds((1 - core) * 512, 512)
@@ -345,61 +370,70 @@
         total[s, own] = value
         pack[s, own] = value.astype(BF)
         for d in (1, 2, 3):
-            x_step(s, d).start()
+            for h in (0, 1):
+                one_step(s, h, d).start()
 
     def sums_y(s):
+        for h in (0, 1):
+            (p, _), _ = order_of(h)
+            for d in (1, 2, 3):
+                one_step(s, h, d).wait()
+            own, cols = pl.ds(core * 512 + p * 128, 128), columns(h)
+            value = total[s, own, cols]
+            for d in (1, 2, 3):
+                value = value + rx[s, h, d - 1].astype(F32)
+            total[s, own, cols] = value
+            pack[s, own, cols] = value.astype(BF)
+            for d in (1, 2, 3):
+                two_step(s, h, d).start()
+
+    def sums_z(s):
+        for h in (0, 1):
+            (p, _), (q, _) = order_of(h)
+            for d in (1, 2, 3):
+                two_step(s, h, d).wait_recv()
+            own = pl.ds(core * 512 + p * 128 + q * 32, 32)
+            value = total[s, own, columns(h)]
+            for d in (1, 2, 3):
+                value = value + ry[s, h, d - 1].astype(F32)
+            rz[s, z, h] = value.astype(BF)
         for d in (1, 2, 3):
-            x_step(s, d).wait()
-        own = pl.ds(core * 512 + x * 128, 128)
-        value = total[s, own] + rx[s, 0].astype(F32) + rx[s, 1].astype(F32) + rx[s, 2].astype(F32)
-        total[s, own] = value
-        pack[s, own] = value.astype(BF)
-        for d in (1, 2, 3):
-            y_step(s, d).start()
-
-    def sums_z(s):
-        for d in (1, 2, 3):
-            y_step(s, d).wait_recv()
-        own = pl.ds(core * 512 + x * 128 + y * 32, 32)
-        value = total[s, own] + ry[s, 0].astype(F32) + ry[s, 1].astype(F32) + ry[s, 2].astype(F32)
-        rz[s, z] = value.astype(BF)
-        for d in (1, 2, 3):
-            z_step(s, d).start()
-
-    def z_landed(s, d):
-        src = rz.at[s, (z + 4 - d) % 4]
-        return remote(src, src, gs.at[s, 3, d - 1], gr.at[s, 3, d - 1], z_ids[d - 1])
+            z_step(s, d, z).start()
 
     def sums_back(s):
         for d in (1, 2, 3):
-            z_landed(s, d).wait_recv()
-        value = rz[s, 0].astype(F32) + rz[s, 1].astype(F32) + rz[s, 2].astype(F32) + rz[s, 3].astype(F32)
-        full[s, pl.ds(core * 512 + x * 128 + y * 32, 32)] = value.astype(BF)
-        for d in (1, 2, 3):
-            spread_step(s, 0, d).start()
-
-    def landed(s, level, d):
-        base, size = (
-            (core * 512 + x * 128 + ((y + 4 - d) % 4) * 32, 32),
-            (core * 512 + ((x + 4 - d) % 4) * 128, 128),
-            ((1 - core) * 512, 512),
-        )[level]
-        rows = full.at[s, pl.ds(base, size)]
-        return remote(rows, rows, gs.at[s, 4 + level, d - 1], gr.at[s, 4 + level, d - 1], sibling)
+            z_step(s, d, (z + 4 - d) % 4).wait_recv()
+        for h in (0, 1):
+            (p, _), (q, _) = order_of(h)
+            value = rz[s, 0, h].astype(F32)
+            for n in (1, 2, 3):
+                value = value + rz[s, n, h].astype(F32)
+            full[s, pl.ds(core * 512 + p * 128 + q * 32, 32), columns(h)] = value.astype(BF)
+            for d in (1, 2, 3):
+                spread_step(s, h, 0, d).start()
 
     def sums_up(s, level):
-        for d in (1, 2, 3):
-            landed(s, level, d).wait_recv()
-        for d in (1, 2, 3) if level == 0 else (1,):
-            spread_step(s, level + 1, d).start()
+        for h in (0, 1):
+            for d in (1, 2, 3):
+                spread_step(s, h, level, d, d).wait_recv()
+            if level == 0:
+                for d in (1, 2, 3):
+                    spread_step(s, h, 1, d).start()
+        if level == 1:
+            half_step(s, core).start()
 
     def sums_end(s):
-        landed(s, 2, 1).wait_recv()
+        half_step(s, 1 - core).wait_recv()
         store = pltpu.make_async_copy(full.at[s], sums_h.at[s], store_sem.at[6 + s])
         store.start()
         return store
 
+    lax.fori_loop(0, 4, functools.partial(later_grads, 0), 0)
+    lax.fori_loop(0, 4, functools.partial(later_grads, 1), 0)
     sums_begin(1)
+    lax.fori_loop(0, 4, functools.partial(later, 0), 0)
+    lax.fori_loop(0, 4, functools.partial(later, 1), 0)
+    sums_x(1)
 
     def last_out(i, c):
         ts = [i * 4 + n for n in range(4)]
@@ -425,13 +459,11 @@
 
     lax.fori_loop(0, 4, early_rest, 0)
     pairs(0, GROUP)
-    sums_x(1)
     lax.fori_loop(0, 8, last_out, 0)
     store_c = pltpu.make_async_copy(cot, out_h.at[1], store_sem.at[2])
     store_c.start()
     store_d = pltpu.make_async_copy(mid.at[pl.ds(LENT, LENT)], grad_h.at[1, pl.ds(LENT, LENT)], store_sem.at[3])
     store_d.start()
-    sums_y(1)
 
     def early(i, c):
         for side in (0, 1):
@@ -445,12 +477,25 @@
 
     lax.fori_loop(0, 8, early, 0)
     sums_begin(0)
-    sums_z(1)
+    sums_y(1)
     store_a.wait()
     pairs(GROUP, PAIRS)
-    lax.fori_loop(0, 8, functools.partial(give_back, 3, send0, ret0), 0)
+
+    def hold_back(j, c):
+        for side in (0, 1):
+            send0[side * 8 + j] = collected(32 + side * 8 + j).astype(BF)
+        return c
+
+    def in_turn(j, c):
+        for side in (0, 1):
+            back(3, send0, ret0, side, j - AHEAD).wait_send()
+            back(3, send0, ret0, side, j).start()
+        return c
+
+    lax.fori_loop(0, AHEAD, functools.partial(give_back, 3, send0, ret0), 0)
     sums_x(0)
-    sums_back(1)
+    lax.fori_loop(AHEAD, 8, hold_back, 0)
+    sums_z(1)
 
     lax.fori_loop(0, LENT, functools.partial(unlent, mid, lent), 0)
     store_e = pltpu.make_async_copy(lent, grad_h.at[1, pl.ds(0, LENT)], store_sem.at[4])
@@ -465,14 +510,21 @@
             put(direct, tiles, straight(0, tiles, stacked(mid, tiles)))
         return c
 
-    lax.fori_loop(0, 4, functools.partial(whole, 1), 0)
+    lax.fori_loop(0, 2, functools.partial(whole, 1), 0)
+    lax.fori_loop(AHEAD, 4, in_turn, 0)
+    sums_back(1)
     sums_y(0)
-    sums_up(1, 0)
-    lax.fori_loop(0, 4, functools.partial(whole, 0), 0)
+    lax.fori_loop(4, 6, in_turn, 0)
+    lax.fori_loop(2, 4, functools.partial(whole, 1), 0)
     store_f = pltpu.make_async_copy(act1.at[pl.ds(LENT, LENT)], grad_h.at[0, pl.ds(LENT, LENT)], store_sem.at[5])
     store_f.start()
+    sums_up(1, 0)
     sums_z(0)
+    lax.fori_loop(6, 8, in_turn, 0)
+    lax.fori_loop(0, 4, functools.partial(whole, 0), 0)
     sums_up(1, 1)
+    sums_back(0)
+    sums_up(0, 0)
 
     def arrive(j, c):
         for side in (0, 1):
@@ -480,7 +532,6 @@
         return c
 
     lax.fori_loop(0, 8, arrive, 0)
-    sums_back(0)
 
     def finish(t, c):
         q = tab[0, t]
@@ -491,7 +542,6 @@
     store_g = pltpu.make_async_copy(act1.at[pl.ds(0, LENT)], grad_h.at[0, pl.ds(0, LENT)], store_sem.at[0])
     store_g.start()
     store_h = sums_end(1)
-    sums_up(0, 0)
     sums_up(0, 1)
     store_i = sums_end(0)
 
@@ -500,19 +550,64 @@
             halo(0, ext0, ext0, side, j).wait_send()
             halo(1, ext1, ext1, side, j).wait_send()
             back(2, send1, ret1, side, j).wait_send()
+        return c
+
+    def drain_last(j, c):
+        for side in (0, 1):
             back(3, send0, ret0, side, j).wait_send()
         return c
 
     lax.fori_loop(0, 8, drain, 0)
+    lax.fori_loop(8 - AHEAD, 8, drain_last, 0)
     for s in (1, 0):
         core_step(s).wait_send()
+        half_step(s, core).wait_send()
         for d in (1, 2, 3):
-            y_step(s, d).wait_send()
-            z_step(s, d).wait_send()
-            spread_step(s, 0, d).wait_send()
-            spread_step(s, 1, d).wait_send()
-        spread_step(s, 2, 1).wait_send()
+            z_step(s, d, z).wait_send()
+            for h in (0, 1):
+                two_step(s, h, d).wait_send()
+                spread_step(s, h, 0, d).wait_send()
+                spread_step(s, h, 1, d).wait_send()
     for copy in (store_b, store_c, store_d, store_e, store_f, store_g, store_h, store_i):
+        copy.wait()
+
+
+CHUNK = 8
+
+
+def deliver(out_m, grad_m, sums_m, out_h, grad_h, self_h, nbr_h, bias_h, wout_h, tiles, sums, wide, bias, get, put):
+    fetch_sums = pltpu.make_async_copy(sums_m, sums, get.at[16])
+    fetch_sums.start()
+    moves = []
+    for a, (src, dst) in enumerate(((out_m, out_h), (grad_m, grad_h))):
+        for s in (0, 1):
+            for c in range(NT // CHUNK):
+                n = (a * 2 + s) * (NT // CHUNK) + c
+                here = tiles.at[n]
+                rows = pl.ds(c * CHUNK, CHUNK)
+                moves.append(
+                    (
+                        pltpu.make_async_copy(src.at[s, rows], here, get.at[n]),
+                        pltpu.make_async_copy(here, dst.at[s, rows], put.at[n]),
+                    )
+                )
+    for fetch, _ in moves:
+        fetch.start()
+    fetch_sums.wait()
+    wide[...] = sums[:, 0 : 3 * HID].astype(F32)
+    for s in (0, 1):
+        bias[s : s + 1, :] = sums[s, 3 * HID : 3 * HID + 1].astype(F32)
+    rest = [pltpu.make_async_copy(bias, bias_h, put.at[16])]
+    for n, dst in enumerate((self_h, nbr_h, wout_h)):
+        rest.append(pltpu.make_async_copy(wide.at[:, pl.ds(n * HID, HID)], dst, put.at[17 + n]))
+    for copy in rest:
+        copy.start()
+    for fetch, store in moves:
+        fetch.wait()
+        store.start()
+    for _, store in moves:
+        store.wait()
+    for copy in rest:
         copy.wait()
 
 
@@ -553,9 +648,9 @@
         pltpu.VMEM((2, GRADS, HID), F32),
         pltpu.VMEM((2, GRADS, HID), BF),
         pltpu.VMEM((2, 512, HID), BF),
-        pltpu.VMEM((2, 3, 128, HID), BF),
-        pltpu.VMEM((2, 3, 32, HID), BF),
-        pltpu.VMEM((2, 4, 32, HID), BF),
+        pltpu.VMEM((2, 2, 3, 128, 128), BF),
+        pltpu.VMEM((2, 2, 3, 32, 128), BF),
+        pltpu.VMEM((2, 4, 2, 32, 128), BF),
         pltpu.VMEM((2, GRADS, HID), BF),
         pltpu.VMEM((8, 128), jnp.int32),
         pltpu.SMEM((8, 128), jnp.int32),
@@ -564,8 +659,8 @@
         dma((8,)),
         dma((4, 2, 8)),
         dma((4, 2, 8)),
-        dma((2, 7, 3)),
-        dma((2, 7, 3)),
+        dma((2, 2, 7, 3)),
+        dma((2, 2, 7, 3)),
     ]
     out, grad, sums = pl.pallas_call(
         mega,
@@ -585,17 +680,39 @@
         name="mesh_layers",
     )(
         node_in.reshape(NT, ROWS, HID), out_cot.reshape(NT, ROWS, HID), adjacency,
-        tile_nbrs, tile_nbrs, bound_tiles, live_tiles, w_self, w_nbr, pre_bias, w_out,
+        tile_nbrs.T, tile_nbrs.T, bound_tiles, live_tiles, w_self, w_nbr, pre_bias, w_out,
     )
+    square = jax.ShapeDtypeStruct((2, HID, HID), F32)
+    out, grad, grad_self, grad_nbr, grad_bias, grad_out = pl.pallas_call(
+        deliver,
+        out_shape=(
+            jax.ShapeDtypeStruct((2, NT, ROWS, HID), BF),
+            jax.ShapeDtypeStruct((2, NT, ROWS, HID), BF),
+            square,
+            square,
+            jax.ShapeDtypeStruct((2, HID), F32),
+            square,
+        ),
+        in_specs=[anyspace] * 3,
+        out_specs=(anyspace,) * 6,
+        scratch_shapes=[
+            pltpu.VMEM((16, CHUNK, ROWS, HID), BF),
+            pltpu.VMEM((2, GRADS, HID), BF),
+            pltpu.VMEM((2, 3 * HID, HID), F32),
+            pltpu.VMEM((2, HID), F32),
+            dma((17,)),
+            dma((20,)),
+        ],
+        name="deliver",
+    )(out, grad, sums)
     rows = NT * ROWS
-    grad_sums = sums.astype(F32)
     return (
         out.reshape(2, rows, HID),
         grad.reshape(2, rows, HID),
-        grad_sums[:, 0:HID],
-        grad_sums[:, HID : 2 * HID],
-        grad_sums[:, 3 * HID],
-        grad_sums[:, 2 * HID : 3 * HID],
+        grad_self,
+        grad_nbr,
+        grad_bias,
+        grad_out,
     )
 
 

time: 135 us -> 105 us (0.78)
  Pallas kernels: 122 us -> 104 us
  local copies, waits for them, and re-layouts: 11.6 us -> 0 us
    pallas_call x1, Pallas kernels: 122 us -> 96.3 us  [per_device(): pl.pallas_call(mega, out_shape=(jax.ShapeDtypeStruct((2, NT, ROWS, HID),...]
    unnamed x6 -> x0, local copies, waits for them, and re-layouts: 8.58 us -> none
    pallas_call x0 -> x1, Pallas kernels: none -> 7.53 us  [per_device(): pl.pallas_call(deliver, out_shape=(jax.ShapeDtypeStruct((2, NT, ROWS, HID...]
    slice x2 -> x0, local copies, waits for them, and re-layouts: 2.98 us -> none  [the longest x1 2.28 us: per_device(): grad_sums[:, 2 * HID:3 * HID]]
where the time goes in v2:
time: 105 us
  Pallas kernels  104 us (99%)
  between operations  1.29 us (1%)
    pallas_call x1, Pallas kernels, per_device(): pl.pallas_call(mega, out_shape=(jax.ShapeDtypeStruct((2, NT, ROWS, HID),...  96.3 us
    pallas_call x1, Pallas kernels, per_device(): pl.pallas_call(deliver, out_shape=(jax.ShapeDtypeStruct((2, NT, ROWS, HID...  7.53 us

profile of v2, /device:TPU:1, one launch (start us, length us, event | category | flops | bytes accessed | tf_op | source)
XLA Modules:
  0.0 105.2 jit_solution(4607894461124636535)
XLA Ops:
  1.3 96.3 %mesh_layers.1 = (bf16[2,32,128,256]{3,2,1,0:T(8,128)(2,1)}, bf16[2,32,128,256]{3,2,1,0:T(8,128)(2,1)}, bf16[2,1024,256]{2,1,0:T(8,128)(2,1)}) custom-call(bf16[32,128,256]{2,1,0:T(8,128)(2,1)} %bitcast.5, bf16[32,128,256]{2,1,0:T(8,128)(2,1)} %bitcast.6, bf16[32,4,128,128]{3,2,1,0:T(8,128)(2,1)} %adj_h.1, s32[4,32]{1,0:T(4,128)} %bitcast.7, ...), custom_call_target="tpu_custom_call" | custom-call | tf_op jit(solution)/shard_map/mesh_layers/pallas_call | solution.py:665
  97.6 7.5 %deliver.1 = (bf16[2,32,128,256]{3,2,1,0:T(8,128)(2,1)}, bf16[2,32,128,256]{3,2,1,0:T(8,128)(2,1)}, f32[2,256,256]{2,1,0:T(8,128)}, f32[2,256,256]{2,1,0:T(8,128...) custom-call(bf16[2,32,128,256]{3,2,1,0:T(8,128)(2,1)} %get-tuple-element.15.out_m, ...), custom_call_target="tpu_custom_call" | custom-call | tf_op jit(solution)/shard_map/deliver/pallas_call | solution.py:686

commit v3 on v2

--- a/solution.py
+++ b/solution.py
@@ -18,7 +18,7 @@
 PAIRS = 96
 GROUP = 48
 GRADS = 1024
-UNROLL = 8
+UNROLL = 16
 AHEAD = 2
 
 
@@ -246,8 +246,8 @@
         put(dagg, tiles, dot(d, w_nbr_t[1]).astype(BF))
         return c
 
-    lax.fori_loop(0, 4, functools.partial(second, 0), 0)
-    lax.fori_loop(0, 4, functools.partial(second, 1), 0)
+    lax.fori_loop(0, 4, functools.partial(second, 0), 0, unroll=2)
+    lax.fori_loop(0, 4, functools.partial(second, 1), 0, unroll=2)
 
     def pair(base, i, c):
         begin = base + i * UNROLL
@@ -321,7 +321,7 @@
         return c
 
     def core_step(s):
-        return remote(pack.at[s, pl.ds((1 - core) * 512, 512)], rc.at[s], gs.at[s, 0, 0, 0], gr.at[s, 0, 0, 0], sibling)
+        return remote(pack.at[s, :, pl.ds((1 - core) * 512, 512)], rc.at[s], gs.at[s, 0, 0, 0], gr.at[s, 0, 0, 0], sibling)
 
     def order_of(h):
         return ((x, x_ids), (y, y_ids)) if h == 0 else ((y, y_ids), (x, x_ids))
@@ -332,13 +332,13 @@
     def one_step(s, h, d):
         (p, ids), _ = order_of(h)
         rows = pl.ds(core * 512 + ((p + d) % 4) * 128, 128)
-        src = pack.at[s, rows, columns(h)]
+        src = pack.at[s, h, rows]
         return remote(src, rx.at[s, h, d - 1], gs.at[s, h, 1, d - 1], gr.at[s, h, 1, d - 1], ids[d - 1])
 
     def two_step(s, h, d):
         (p, _), (q, ids) = order_of(h)
         rows = pl.ds(core * 512 + p * 128 + ((q + d) % 4) * 32, 32)
-        src = pack.at[s, rows, columns(h)]
+        src = pack.at[s, h, rows]
         return remote(src, ry.at[s, h, d - 1], gs.at[s, h, 2, d - 1], gr.at[s, h, 2, d - 1], ids[d - 1])
 
     def z_step(s, d, slot):
@@ -351,24 +351,26 @@
             base, size, ids = core * 512 + p * 128 + ((q + 4 - back_by) % 4) * 32, 32, ids_q
         else:
             base, size, ids = core * 512 + ((p + 4 - back_by) % 4) * 128, 128, ids_p
-        rows = full.at[s, pl.ds(base, size), columns(h)]
+        rows = full.at[s, h, pl.ds(base, size)]
         return remote(rows, rows, gs.at[s, h, 4 + level, d - 1], gr.at[s, h, 4 + level, d - 1], ids[d - 1])
 
     def half_step(s, half):
-        rows = full.at[s, pl.ds(half * 512, 512)]
+        rows = full.at[s, :, pl.ds(half * 512, 512)]
         return remote(rows, rows, gs.at[s, 0, 6, 0], gr.at[s, 0, 6, 0], sibling)
 
     def sums_begin(s):
         other = pl.ds((1 - core) * 512, 512)
-        pack[s, other] = total[s, other].astype(BF)
+        for h in (0, 1):
+            pack[s, h, other] = total[s, other, columns(h)].astype(BF)
         core_step(s).start()
 
     def sums_x(s):
         core_step(s).wait_recv()
         own = pl.ds(core * 512, 512)
-        value = total[s, own] + rc[s].astype(F32)
-        total[s, own] = value
-        pack[s, own] = value.astype(BF)
+        for h in (0, 1):
+            value = total[s, own, columns(h)] + rc[s, h].astype(F32)
+            total[s, own, columns(h)] = value
+            pack[s, h, own] = value.astype(BF)
         for d in (1, 2, 3):
             for h in (0, 1):
                 one_step(s, h, d).start()
@@ -383,7 +385,7 @@
             for d in (1, 2, 3):
                 value = value + rx[s, h, d - 1].astype(F32)
             total[s, own, cols] = value
-            pack[s, own, cols] = value.astype(BF)
+            pack[s, h, own] = value.astype(BF)
             for d in (1, 2, 3):
                 two_step(s, h, d).start()
 
@@ -408,7 +410,7 @@
             value = rz[s, 0, h].astype(F32)
             for n in (1, 2, 3):
                 value = value + rz[s, n, h].astype(F32)
-            full[s, pl.ds(core * 512 + p * 128 + q * 32, 32), columns(h)] = value.astype(BF)
+            full[s, h, pl.ds(core * 512 + p * 128 + q * 32, 32)] = value.astype(BF)
             for d in (1, 2, 3):
                 spread_step(s, h, 0, d).start()
 
@@ -495,7 +497,6 @@
     lax.fori_loop(0, AHEAD, functools.partial(give_back, 3, send0, ret0), 0)
     sums_x(0)
     lax.fori_loop(AHEAD, 8, hold_back, 0)
-    sums_z(1)
 
     lax.fori_loop(0, LENT, functools.partial(unlent, mid, lent), 0)
     store_e = pltpu.make_async_copy(lent, grad_h.at[1, pl.ds(0, LENT)], store_sem.at[4])
@@ -512,18 +513,18 @@
 
     lax.fori_loop(0, 2, functools.partial(whole, 1), 0)
     lax.fori_loop(AHEAD, 4, in_turn, 0)
-    sums_back(1)
     sums_y(0)
     lax.fori_loop(4, 6, in_turn, 0)
     lax.fori_loop(2, 4, functools.partial(whole, 1), 0)
     store_f = pltpu.make_async_copy(act1.at[pl.ds(LENT, LENT)], grad_h.at[0, pl.ds(LENT, LENT)], store_sem.at[5])
     store_f.start()
-    sums_up(1, 0)
+    sums_z(1)
     sums_z(0)
     lax.fori_loop(6, 8, in_turn, 0)
     lax.fori_loop(0, 4, functools.partial(whole, 0), 0)
-    sums_up(1, 1)
+    sums_back(1)
     sums_back(0)
+    sums_up(1, 0)
     sums_up(0, 0)
 
     def arrive(j, c):
@@ -541,8 +542,9 @@
     lax.fori_loop(0, LENT, finish, 0)
     store_g = pltpu.make_async_copy(act1.at[pl.ds(0, LENT)], grad_h.at[0, pl.ds(0, LENT)], store_sem.at[0])
     store_g.start()
+    sums_up(1, 1)
+    sums_up(0, 1)
     store_h = sums_end(1)
-    sums_up(0, 1)
     store_i = sums_end(0)
 
     def drain(j, c):
@@ -594,9 +596,11 @@
     for fetch, _ in moves:
         fetch.start()
     fetch_sums.wait()
-    wide[...] = sums[:, 0 : 3 * HID].astype(F32)
-    for s in (0, 1):
-        bias[s : s + 1, :] = sums[s, 3 * HID : 3 * HID + 1].astype(F32)
+    for h in (0, 1):
+        cols = pl.ds(h * 128, 128)
+        wide[:, :, cols] = sums[:, h, 0 : 3 * HID].astype(F32)
+        for s in (0, 1):
+            bias[s : s + 1, cols] = sums[s, h, 3 * HID : 3 * HID + 1].astype(F32)
     rest = [pltpu.make_async_copy(bias, bias_h, put.at[16])]
     for n, dst in enumerate((self_h, nbr_h, wout_h)):
         rest.append(pltpu.make_async_copy(wide.at[:, pl.ds(n * HID, HID)], dst, put.at[17 + n]))
@@ -646,12 +650,12 @@
         pltpu.VMEM((2, HID, HID), BF),
         pltpu.VMEM((2, HID, HID), BF),
         pltpu.VMEM((2, GRADS, HID), F32),
-        pltpu.VMEM((2, GRADS, HID), BF),
-        pltpu.VMEM((2, 512, HID), BF),
+        pltpu.VMEM((2, 2, GRADS, 128), BF),
+        pltpu.VMEM((2, 2, 512, 128), BF),
         pltpu.VMEM((2, 2, 3, 128, 128), BF),
         pltpu.VMEM((2, 2, 3, 32, 128), BF),
         pltpu.VMEM((2, 4, 2, 32, 128), BF),
-        pltpu.VMEM((2, GRADS, HID), BF),
+        pltpu.VMEM((2, 2, GRADS, 128), BF),
         pltpu.VMEM((8, 128), jnp.int32),
         pltpu.SMEM((8, 128), jnp.int32),
         dma((9,)),
@@ -667,7 +671,7 @@
         out_shape=(
             jax.ShapeDtypeStruct((2, NT, ROWS, HID), BF),
             jax.ShapeDtypeStruct((2, NT, ROWS, HID), BF),
-            jax.ShapeDtypeStruct((2, GRADS, HID), BF),
+            jax.ShapeDtypeStruct((2, 2, GRADS, 128), BF),
         ),
         in_specs=[
             anyspace, anyspace, anyspace, vmem, smem, smem, smem, anyspace, anyspace, vmem, anyspace,
@@ -697,7 +701,7 @@
         out_specs=(anyspace,) * 6,
         scratch_shapes=[
             pltpu.VMEM((16, CHUNK, ROWS, HID), BF),
-            pltpu.VMEM((2, GRADS, HID), BF),
+            pltpu.VMEM((2, 2, GRADS, 128), BF),
             pltpu.VMEM((2, 3 * HID, HID), F32),
             pltpu.VMEM((2, HID), F32),
             dma((17,)),

time: 105 us -> 100 us (0.952)
  Pallas kernels: 104 us -> 98.7 us
    pallas_call x1, Pallas kernels: 96.3 us -> 91.2 us  [per_device(): pl.pallas_call(mega, out_shape=(jax.ShapeDtypeStruct((2, NT, ROWS, HID),...]
where the time goes in v3:
time: 100 us
  Pallas kernels  98.7 us (99%)
  between operations  1.29 us (1%)
    pallas_call x1, Pallas kernels, per_device(): pl.pallas_call(mega, out_shape=(jax.ShapeDtypeStruct((2, NT, ROWS, HID),...  91.2 us
    pallas_call x1, Pallas kernels, per_device(): pl.pallas_call(deliver, out_shape=(jax.ShapeDtypeStruct((2, NT, ROWS, HID...  7.53 us

profile of v3, /device:TPU:1, one launch (start us, length us, event | category | flops | bytes accessed | tf_op | source)
XLA Modules:
  0.0 100.0 jit_solution(7141496610925893602)
XLA Ops:
  1.3 91.2 %mesh_layers.1 = (bf16[2,32,128,256]{3,2,1,0:T(8,128)(2,1)}, bf16[2,32,128,256]{3,2,1,0:T(8,128)(2,1)}, bf16[2,2,1024,128]{3,2,1,0:T(8,128)(2,1)}) custom-call(bf16[32,128,256]{2,1,0:T(8,128)(2,1)} %bitcast.5, bf16[32,128,256]{2,1,0:T(8,128)(2,1)} %bitcast.6, bf16[32,4,128,128]{3,2,1,0:T(8,128)(2,1)} %adj_h.1, s32[4,32]{1,0:T(4,128)} %bitcast.7, ...), custom_call_target="tpu_custom_call" | custom-call | tf_op jit(solution)/shard_map/mesh_layers/pallas_call | solution.py:669
  92.5 7.5 %deliver.1 = (bf16[2,32,128,256]{3,2,1,0:T(8,128)(2,1)}, bf16[2,32,128,256]{3,2,1,0:T(8,128)(2,1)}, f32[2,256,256]{2,1,0:T(8,128)}, f32[2,256,256]{2,1,0:T(8,128...) custom-call(bf16[2,32,128,256]{3,2,1,0:T(8,128)(2,1)} %get-tuple-element.15.out_m, ...), custom_call_target="tpu_custom_call" | custom-call | tf_op jit(solution)/shard_map/deliver/pallas_call | solution.py:690

commit v4 on v3

--- a/solution.py
+++ b/solution.py
@@ -18,7 +18,7 @@
 PAIRS = 96
 GROUP = 48
 GRADS = 1024
-UNROLL = 16
+UNROLL = 48
 AHEAD = 2
 
 
@@ -96,6 +96,11 @@
     y_ids = [chip_id(x, (y + d) % 4, core, z) for d in (1, 2, 3)]
     z_ids = [chip_id(x, y, core, (z + d) % 4) for d in (1, 2, 3)]
 
+    barrier = pltpu.get_barrier_semaphore()
+    greeted = [west, east, sibling, *x_ids, *y_ids, *z_ids]
+    for device in greeted:
+        pl.semaphore_signal(barrier, inc=1, device_id=device, device_id_type=MESH)
+
     loads = [
         pltpu.make_async_copy(node_h.at[pl.ds(0, LENT)], lent, load_sem.at[0]),
         pltpu.make_async_copy(node_h.at[pl.ds(LENT, LENT)], ext0.at[pl.ds(LENT, LENT)], load_sem.at[1]),
@@ -110,10 +115,6 @@
     for copy in loads:
         copy.start()
 
-    barrier = pltpu.get_barrier_semaphore()
-    greeted = [west, east, sibling, *x_ids, *y_ids, *z_ids]
-    for device in greeted:
-        pl.semaphore_signal(barrier, inc=1, device_id=device, device_id_type=MESH)
     pl.semaphore_wait(barrier, len(greeted))
 
     def remote(src, dst, ssem, rsem, device):
@@ -246,8 +247,8 @@
         put(dagg, tiles, dot(d, w_nbr_t[1]).astype(BF))
         return c
 
-    lax.fori_loop(0, 4, functools.partial(second, 0), 0, unroll=2)
-    lax.fori_loop(0, 4, functools.partial(second, 1), 0, unroll=2)
+    lax.fori_loop(0, 4, functools.partial(second, 0), 0, unroll=4)
+    lax.fori_loop(0, 4, functools.partial(second, 1), 0, unroll=4)
 
     def pair(base, i, c):
         begin = base + i * UNROLL
@@ -574,11 +575,12 @@
         copy.wait()
 
 
-CHUNK = 8
+CHUNK = 16
+CHUNKS = 4 * NT // CHUNK
 
 
 def deliver(out_m, grad_m, sums_m, out_h, grad_h, self_h, nbr_h, bias_h, wout_h, tiles, sums, wide, bias, get, put):
-    fetch_sums = pltpu.make_async_copy(sums_m, sums, get.at[16])
+    fetch_sums = pltpu.make_async_copy(sums_m, sums, get.at[CHUNKS])
     fetch_sums.start()
     moves = []
     for a, (src, dst) in enumerate(((out_m, out_h), (grad_m, grad_h))):
@@ -601,9 +603,9 @@
         wide[:, :, cols] = sums[:, h, 0 : 3 * HID].astype(F32)
         for s in (0, 1):
             bias[s : s + 1, cols] = sums[s, h, 3 * HID : 3 * HID + 1].astype(F32)
-    rest = [pltpu.make_async_copy(bias, bias_h, put.at[16])]
+    rest = [pltpu.make_async_copy(bias, bias_h, put.at[CHUNKS])]
     for n, dst in enumerate((self_h, nbr_h, wout_h)):
-        rest.append(pltpu.make_async_copy(wide.at[:, pl.ds(n * HID, HID)], dst, put.at[17 + n]))
+        rest.append(pltpu.make_async_copy(wide.at[:, pl.ds(n * HID, HID)], dst, put.at[CHUNKS + 1 + n]))
     for copy in rest:
         copy.start()
     for fetch, store in moves:
@@ -700,12 +702,12 @@
         in_specs=[anyspace] * 3,
         out_specs=(anyspace,) * 6,
         scratch_shapes=[
-            pltpu.VMEM((16, CHUNK, ROWS, HID), BF),
+            pltpu.VMEM((CHUNKS, CHUNK, ROWS, HID), BF),
             pltpu.VMEM((2, 2, GRADS, 128), BF),
             pltpu.VMEM((2, 3 * HID, HID), F32),
             pltpu.VMEM((2, HID), F32),
-            dma((17,)),
-            dma((20,)),
+            dma((CHUNKS + 1,)),
+            dma((CHUNKS + 4,)),
         ],
         name="deliver",
     )(out, grad, sums)

time: 100 us -> 97.7 us (0.977)
  Pallas kernels: 98.7 us -> 96.1 us
    pallas_call x1, Pallas kernels: 91.2 us -> 88.8 us  [per_device(): pl.pallas_call(mega, out_shape=(jax.ShapeDtypeStruct((2, NT, ROWS, HID),...]
where the time goes in v4:
time: 97.7 us; the launch traced here: 97.5 us
  Pallas kernels  96.1 us (98%)
  between operations  1.45 us (1%)
    pallas_call x1, Pallas kernels, per_device(): pl.pallas_call(mega, out_shape=(jax.ShapeDtypeStruct((2, NT, ROWS, HID),...  88.8 us
    pallas_call x1, Pallas kernels, per_device(): pl.pallas_call(deliver, out_shape=(jax.ShapeDtypeStruct((2, NT, ROWS, HID...  7.31 us

profile of v4, /device:TPU:1, one launch (start us, length us, event | category | flops | bytes accessed | tf_op | source)
XLA Modules:
  0.0 97.5 jit_solution(7034099475774560367)
XLA Ops:
  1.3 88.8 %mesh_layers.1 = (bf16[2,32,128,256]{3,2,1,0:T(8,128)(2,1)}, bf16[2,32,128,256]{3,2,1,0:T(8,128)(2,1)}, bf16[2,2,1024,128]{3,2,1,0:T(8,128)(2,1)}) custom-call(bf16[32,128,256]{2,1,0:T(8,128)(2,1)} %bitcast.5, bf16[32,128,256]{2,1,0:T(8,128)(2,1)} %bitcast.6, bf16[32,4,128,128]{3,2,1,0:T(8,128)(2,1)} %adj_h.1, s32[4,32]{1,0:T(4,128)} %bitcast.7, ...), custom_call_target="tpu_custom_call" | custom-call | tf_op jit(solution)/shard_map/mesh_layers/pallas_call | solution.py:671
  90.0 7.3 %deliver.1 = (bf16[2,32,128,256]{3,2,1,0:T(8,128)(2,1)}, bf16[2,32,128,256]{3,2,1,0:T(8,128)(2,1)}, f32[2,256,256]{2,1,0:T(8,128)}, f32[2,256,256]{2,1,0:T(8,128...) custom-call(bf16[2,32,128,256]{3,2,1,0:T(8,128)(2,1)} %get-tuple-element.15.out_m, ...), custom_call_target="tpu_custom_call" | custom-call | tf_op jit(solution)/shard_map/deliver/pallas_call | solution.py:692
